TPU v7x, 256 devices: a whole 4x4x8 slice. The times are simulated.
256 devices in a mesh: dp: 16 (over y_hi, x, core), tm: 16 (over y_lo, z).
Axes of the slice: x: 4, y: 4 (y_hi: 2, y_lo: 2; y = y_hi * 2 + y_lo), z: 8, core: 2. Of those that a mesh axis runs over, the one named last changes fastest.
Arguments:
- query_rows: bfloat16 [16, 3584, 1024], P('dp', 'tm'), may hold values from -6 to 6
- key_rows: bfloat16 [16, 3584, 1024], P('dp', 'tm'), may hold values from -6 to 6
- value_rows: bfloat16 [16, 3584, 1024], P('dp', 'tm'), may hold values from -6 to 6
- head_scale: float32 [16], replicated, may hold values from 2 to 16
- out_proj: bfloat16 [1024, 1536], replicated, may hold values from -0.1875 to 0.1875
- conv_taps: float32 [31, 1536], replicated, may hold values from -1 to 1
- router: bfloat16 [1536, 16], replicated, may hold values from -0.15625 to 0.15625
- expert_in: bfloat16 [16, 2048, 1536], P('dp', 'tm'), may hold values from -0.15625 to 0.15625
- expert_out: bfloat16 [16, 2048, 1536], P('dp', 'tm'), may hold values from -0.125 to 0.125
- lengths: int32 [16, 4], P('dp'), may hold values from 1 to 2688, 3584 in all within a row
- routes: int32 [16, 3584, 2], P('dp', 'tm'), may hold values from 0 to 15, all different within a row; in each aligned block of 224 rows (0 to 223, 224 to 447, ..., all dimensions but the last counted through in order) at most 42 rows name the same one
Outputs:
- block_out: bfloat16 [16, 3584, 1536], P('dp', 'tm')
Inputs may be any that keep to these rules, and one draw needn't show every extreme that they name: Every length is at least 1, the 4 lengths of a pack sum to 3584, and the largest of each pack is exactly 2688. `routes`: the 2 experts of a frame differ. Among the 224 frames of one block (frames j * 224 to (j + 1) * 224 - 1 of a pack), no expert is named by more than 42 frames, and in some block some expert is named by exactly 42. Every expert is named somewhere.
All inputs are finite; a program needn't handle non-finite values.
Results may differ from a plain program's by a relative error of at most 0.0099.
Values may be sent and summed in bfloat16 or wider, within the bound.
A program may use at most 128 MiB of HBM per device.

v0:
```python
import jax
import jax.numpy as jnp
from jax import lax
from jax.sharding import PartitionSpec as P

D = 1536
HEADS = 16
HEAD_DIM = 64
KERNEL = 31
TOPK = 2
RECS = 4


def with_halo(cells, sides, width):
    for axis, dim in sides:
        count = lax.axis_size(axis)
        ends = count - 1
        head = lax.slice_in_dim(cells, 0, width, axis=dim)
        tail = lax.slice_in_dim(cells, cells.shape[dim] - width, cells.shape[dim], axis=dim)
        cells = jnp.concatenate(
            [
                lax.ppermute(tail, axis, [(i, (i + 1) % count) for i in range(ends)]),
                cells,
                lax.ppermute(head, axis, [((i + 1) % count, i) for i in range(ends)]),
            ],
            axis=dim,
        )
    return cells


def layer_norm(values):
    average = jnp.mean(values, axis=-1, keepdims=True)
    centered = values - average
    spread = jnp.mean(centered * centered, axis=-1, keepdims=True)
    return centered * lax.rsqrt(spread + 1e-05)


def unit_heads(rows):
    lifted = rows.astype(jnp.float32).reshape(rows.shape[0], HEADS, HEAD_DIM)
    factor = lax.rsqrt(jnp.sum(lifted * lifted, axis=-1, keepdims=True) + 1e-06)
    return (lifted * factor).astype(jnp.bfloat16)


def recording_of(positions, pack_lengths):
    bounds = jnp.cumsum(pack_lengths)[: RECS - 1]
    return jnp.sum((positions[:, None] >= bounds[None, :]).astype(jnp.int32), axis=1)


def add_scores(query_heads, own_labels, piece_keys, piece_values, piece_labels, head_scale):
    count = piece_keys.shape[0]
    key_heads = jnp.transpose(piece_keys.reshape(count, HEADS, HEAD_DIM), (1, 0, 2))
    value_heads = jnp.transpose(piece_values.reshape(count, HEADS, HEAD_DIM), (1, 0, 2))
    inside = own_labels[:, None] == piece_labels[None, :]

    def per_head(items):
        query_one, key_one, value_one, scale = items
        scores = lax.dot_general(
            query_one, key_one, (((1,), (1,)), ((), ())), preferred_element_type=jnp.float32
        )
        weights = jnp.where(inside, jnp.exp(scale * (scores - 1.0)), 0.0)
        weight_sum = jnp.sum(weights, axis=1)
        product = jnp.dot(
            weights.astype(jnp.bfloat16), value_one, preferred_element_type=jnp.float32
        )
        return (product, weight_sum)

    products, weight_sums = lax.map(per_head, (query_heads, key_heads, value_heads, head_scale))
    return (products, weight_sums)


def body(
    query_rows,
    key_rows,
    value_rows,
    head_scale,
    out_proj,
    conv_taps,
    router,
    expert_in,
    expert_out,
    lengths,
    routes,
):
    row_count = query_rows.shape[1]
    experts = lax.axis_size("dp")
    capacity = 3 * row_count // experts
    offset = lax.axis_index("tm") * row_count
    pack_lengths = lengths[0]
    own_labels = recording_of(offset + jnp.arange(row_count, dtype=jnp.int32), pack_lengths)
    query_heads = jnp.transpose(unit_heads(query_rows[0]), (1, 0, 2))
    key_unit = unit_heads(key_rows[0]).reshape(row_count, HEADS * HEAD_DIM)
    piece_keys = lax.all_gather(key_unit, "tm", axis=0, tiled=True)
    piece_values = lax.all_gather(value_rows[0], "tm", axis=0, tiled=True)
    count = piece_keys.shape[0]
    piece_labels = recording_of(jnp.arange(count, dtype=jnp.int32), pack_lengths)
    sums, masses = add_scores(
        query_heads, own_labels, piece_keys, piece_values, piece_labels, head_scale
    )
    attended = (
        jnp.transpose(sums / masses[:, :, None], (1, 0, 2))
        .reshape(row_count, HEADS * HEAD_DIM)
        .astype(jnp.bfloat16)
    )
    first = jnp.dot(attended, out_proj, preferred_element_type=jnp.float32)
    normed = layer_norm(first).astype(jnp.bfloat16)
    half = (KERNEL - 1) // 2
    padded = with_halo(normed, (("tm", 0),), half)
    padded_labels = recording_of(
        offset - half + jnp.arange(row_count + 2 * half, dtype=jnp.int32), pack_lengths
    )
    total = jnp.zeros((row_count, D), jnp.float32)
    for tap in range(KERNEL):
        same = (padded_labels[tap : tap + row_count] == own_labels)[:, None]
        term = conv_taps[tap][None, :] * padded[tap : tap + row_count].astype(jnp.float32)
        total = total + jnp.where(same, term, 0.0)
    second = first + jax.nn.silu(total)
    mixed_in = layer_norm(second).astype(jnp.bfloat16)
    logits = jnp.dot(mixed_in, router, preferred_element_type=jnp.float32)
    own_routes = routes[0]
    chosen = jnp.exp(jnp.take_along_axis(logits, own_routes, axis=1))
    gates = chosen / jnp.sum(chosen, axis=1, keepdims=True)
    picks = jnp.sum(
        (own_routes[:, :, None] == jnp.arange(experts, dtype=jnp.int32)).astype(jnp.int32), axis=1
    )
    ranks = jnp.cumsum(picks, axis=0) - picks
    slots = own_routes * capacity + jnp.take_along_axis(ranks, own_routes, axis=1)
    placing = jnp.sum(
        (slots[:, :, None] == jnp.arange(experts * capacity, dtype=jnp.int32)).astype(jnp.bfloat16),
        axis=1,
    )
    outgoing = lax.dot_general(
        placing, mixed_in, (((0,), (0,)), ((), ())), preferred_element_type=jnp.float32
    )
    outgoing = outgoing.astype(jnp.bfloat16).reshape(experts, capacity, D)
    arrived = lax.all_to_all(outgoing, "dp", split_axis=0, concat_axis=0, tiled=True).reshape(
        experts * capacity, D
    )
    piece_in = lax.all_gather(expert_in[0], "tm", axis=0, tiled=True)
    piece_out = lax.all_gather(expert_out[0], "tm", axis=0, tiled=True)
    hidden_part = jax.nn.silu(
        lax.dot_general(
            arrived, piece_in, (((1,), (1,)), ((), ())), preferred_element_type=jnp.float32
        )
    ).astype(jnp.bfloat16)
    produced = jnp.dot(hidden_part, piece_out, preferred_element_type=jnp.float32)
    returned = lax.all_to_all(
        produced.astype(jnp.bfloat16).reshape(experts, capacity, D),
        "dp",
        split_axis=0,
        concat_axis=0,
        tiled=True,
    )
    returned = returned.reshape(experts * capacity, D)
    mixture = jnp.zeros((row_count, D), jnp.float32)
    for pick in range(TOPK):
        mixture = mixture + gates[:, pick : pick + 1] * returned[slots[:, pick]].astype(jnp.float32)
    return (second + 0.5 * mixture).astype(jnp.bfloat16)[None]


def solution(mesh):
    return jax.shard_map(
        body,
        mesh=mesh,
        in_specs=(
            P("dp", "tm", None),
            P("dp", "tm", None),
            P("dp", "tm", None),
            P(),
            P(),
            P(),
            P(),
            P("dp", "tm", None),
            P("dp", "tm", None),
            P("dp", None),
            P("dp", "tm", None),
        ),
        out_specs=P("dp", "tm", None),
        check_vma=False,
    )
```

profile of v0, /device:TPU:1, one launch (start us, length us, event | category | flops | bytes accessed | tf_op | source)
XLA Modules:
  0.0 462.5 jit_solution(16860183570171836455)
XLA Ops:
  30.8 3.2 gather_fusion.3
  34.9 75.4 %all-gather.8.cloned.1.call-done = bf16[3584,1024]{1,0:T(8,128)(2,1)} async-done(((bf16[224,1024]{1,0:T(8,128)(2,1)}), bf16[3584,1024]{1,0:T(8,128)(2,1)}) %all-gather.8.cloned.1.call-update) | async-done | bytes 7340048 | tf_op jit(solution)/shard_map/all_gather | solution.py:92
  110.4 10.0 %copy.56 = bf16[3584,1024]{0,1:T(8,128)(2,1)} copy(bf16[3584,1024]{1,0:T(8,128)(2,1)} %all-gather.8.cloned.1.call-done) | data formatting | bytes 14680064 | tf_op jit(solution)/shard_map/all_gather | solution.py:92
  120.4 79.9 %all-gather.10.cloned.1.call-done = bf16[1,3584,1024]{2,1,0:T(8,128)(2,1)} async-done(((bf16[1,224,1024]{2,1,0:T(8,128)(2,1)}), bf16[1,3584,1024]{2,1,0:T(8,128)(2,1)}) %all-gather.10.cloned.1.call-update) | async-done | bytes 7340048 | tf_op jit(solution)/shard_map/all_gather | solution.py:93
  200.3 10.1 %copy.57 = bf16[1,3584,1024]{1,2,0:T(8,128)(2,1)} copy(bf16[1,3584,1024]{2,1,0:T(8,128)(2,1)} %all-gather.10.cloned.1.call-done) | data formatting | bytes 14680064 | tf_op jit(solution)/shard_map/all_gather | solution.py:93
  210.4 93.1 %while.15 = (s32[]{:T(128)}, f32[16,224,64]{1,2,0:T(8,128)}, f32[16,224]{1,0:T(8,128)S(1)}, f32[16]{0:T(128)S(1)}, bf16[16,224,64]{1,2,0:T(8,128)(2,1)}, /*index...) while((s32[]{:T(128)}, f32[16,224,64]{1,2,0:T(8,128)}, ...), condition=%wide.region_7.8_spmd.clone, body=%wide.region_5.7_spmd.clone.sunk | while | flops 210337568 | bytes 4247677 | solution.py:67
  211.1 2.8 fusion.96
  216.9 2.8 fusion.96
  222.7 2.9 fusion.96
  228.6 2.9 fusion.96
  234.4 2.9 fusion.96
  240.2 2.9 fusion.96
  246.0 2.8 fusion.96
  251.8 2.9 fusion.96
  257.7 2.9 fusion.96
  263.5 2.9 fusion.96
  269.3 2.9 fusion.96
  275.1 2.8 fusion.96
  280.9 2.8 fusion.96
  286.7 2.9 fusion.96
  292.5 2.9 fusion.96
  298.3 2.9 fusion.96
  310.1 4.3 collective-permute-done.1
  314.7 17.4 %fusion.77 = (f32[224]{0:T(256)S(1)}, f32[224,1536]{1,0:T(8,128)S(1)}) fusion(f32[224,1536]{1,0:T(8,128)S(1)} %get-tuple-element.258, bf16[15,1536]{1,0:T(8,128)(2,1)S(1)} %collective-permute-done.1, bf16[224,1536]{1,0:T(8,128)(2,1)S(1)} %multiply_convert_fusion.3, f32[1536]{0:T(1024)S(1)} %copy-done.29, pred[224]{0:T(512)(128)(4,1)S(1)} %copy-done.38, ...), kind=kLoop, calls=%fused_computation.226 | loop fusion | flops 75349792 | bytes 3731104 | tf_op jit(solution)/shard_map/reduce_sum | solution.py:32
  337.9 50.4 %all_to_all.10 = bf16[16,42,1536]{2,1,0:T(8,128)(2,1)} all-to-all(bf16[16,42,1536]{2,1,0:T(8,128)(2,1)S(1)} %reshape.193), channel_id=1, replica_groups=mesh['dp'=16,'tm'=16] {'dp'}, dimensions={0} | all-to-all | bytes 4128768 | tf_op jit(solution)/shard_map/all_to_all | solution.py:135
  388.2 2.7 reshape.194
  391.0 14.9 %fusion.25 = bf16[672,1536]{1,0:T(8,128)(2,1)} fusion(bf16[1,2048,1536]{2,1,0:T(8,128)(2,1)} %all-gather.14.cloned.1.call-done, bf16[672,1536]{1,0:T(8,128)(2,1)S(1)} %reshape.194, bf16[1,2048,1536]{2,1,0:T(8,128)(2,1)} %all-gather.12.cloned.1.call-done), kind=kOutput, calls=%fused_computation.54 | convolution fusion | flops 8463630336 | bytes 16711680 | tf_op jit(solution)/shard_map/dot_general | solution.py:145
  405.8 4.0 reshape.195
  409.9 4.8 %all-to-all-start.1 = ((bf16[16,42,1536]{2,1,0:T(8,128)(2,1)}), bf16[16,42,1536]{2,1,0:T(8,128)(2,1)}, u32[]{:S(2)}, u32[]{:S(2)}) async-start(bf16[16,42,1536]{2,1,0:T(8,128)(2,1)} %reshape.195), calls=%async_computation.1 | async-start | bytes 4718592 | tf_op jit(solution)/shard_map/all_to_all | solution.py:146
  415.2 4.0 gather_fusion.2
  419.7 26.4 %all-to-all-done.1 = bf16[16,42,1536]{2,1,0:T(8,128)(2,1)} async-done(((bf16[16,42,1536]{2,1,0:T(8,128)(2,1)}), bf16[16,42,1536]{2,1,0:T(8,128)(2,1)}, u32[]{:S(2)}, u32[]{:S(2)}) %all-to-all-start.1) | async-done | bytes 2064416 | tf_op jit(solution)/shard_map/all_to_all | solution.py:146
  452.8 3.1 fusion.39
  (230 shorter events, 92.0 us)
Async XLA Ops:
  6.5 298.3 %copy-start = (bf16[1024,1536]{1,0:T(8,128)(2,1)S(1)}, bf16[1024,1536]{1,0:T(8,128)(2,1)}, u32[]{:S(2)}) copy-start(bf16[1024,1536]{1,0:T(8,128)(2,1)} %param.17) | copy-start | bytes 9437188
  6.5 103.8 %all-gather.8.cloned.1.call-start = ((), (), s32[]{:S(2)}) async-start(), calls=%async_computation.2 | async-start | bytes 7798784 | tf_op jit(solution)/shard_map/all_gather | solution.py:92
  14.1 8.4 %copy-start.36 = (s32[1,224,2]{1,2,0:T(2,128)S(1)}, s32[1,224,2]{1,2,0:T(2,128)}, u32[]{:S(2)}) copy-start(s32[1,224,2]{1,2,0:T(2,128)} %param.23) | copy-start | bytes 5380
  16.2 184.1 %all-gather.10.cloned.1.call-start = ((), (), s32[]{:S(2)}) async-start(), calls=%async_computation.3 | async-start | bytes 7798784 | tf_op jit(solution)/shard_map/all_gather | solution.py:93
  16.9 374.0 %all-gather.12.cloned.1.call-start = ((), (), s32[]{:S(2)}) async-start(), calls=%async_computation.4 | async-start | bytes 6684672 | tf_op jit(solution)/shard_map/all_gather | solution.py:138
  17.7 373.3 %all-gather.14.cloned.1.call-start = ((), (), s32[]{:S(2)}) async-start(), calls=%async_computation.5 | async-start | bytes 6684672 | tf_op jit(solution)/shard_map/all_gather | solution.py:139
  120.4 90.0 %copy-start.31 = (f32[16,224]{1,0:T(8,128)S(1)}, f32[16,224]{1,0:T(8,128)}, u32[]{:S(2)}) copy-start(f32[16,224]{1,0:T(8,128)} %custom-call.9) | copy-start | bytes 43012
  120.4 90.0 %copy-start.32 = (s32[3584]{0:T(1024)S(1)}, s32[3584]{0:T(1024)}, u32[]{:S(2)}) copy-start(s32[3584]{0:T(1024)} %convert_reduce_fusion) | copy-start | bytes 43012
  120.4 90.0 %copy-start.34 = (s32[224]{0:T(256)S(1)}, s32[224]{0:T(256)}, u32[]{:S(2)}) copy-start(s32[224]{0:T(256)} %copy-done.33) | copy-start | bytes 2692
  120.4 90.0 %copy-start.51 = (f32[16]{0:T(128)S(1)}, f32[16]{0:T(128)}, u32[]{:S(2)}) copy-start(f32[16]{0:T(128)} %param.16) | copy-start | bytes 196
  306.1 8.2 %copy-start.5 = (f32[1536]{0:T(1024)S(1)}, f32[1536]{0:T(1024)}, u32[]{:S(2)}) copy-start(f32[1536]{0:T(1024)} %get-tuple-element.172) | copy-start | bytes 18436
  306.2 8.2 %copy-start.6 = (f32[1536]{0:T(1024)S(1)}, f32[1536]{0:T(1024)}, u32[]{:S(2)}) copy-start(f32[1536]{0:T(1024)} %get-tuple-element.173) | copy-start | bytes 18436
  306.2 8.2 %copy-start.7 = (f32[1536]{0:T(1024)S(1)}, f32[1536]{0:T(1024)}, u32[]{:S(2)}) copy-start(f32[1536]{0:T(1024)} %get-tuple-element.174) | copy-start | bytes 18436
  306.2 8.2 %copy-start.8 = (f32[1536]{0:T(1024)S(1)}, f32[1536]{0:T(1024)}, u32[]{:S(2)}) copy-start(f32[1536]{0:T(1024)} %get-tuple-element.175) | copy-start | bytes 18436
  306.2 8.2 %copy-start.9 = (f32[1536]{0:T(1024)S(1)}, f32[1536]{0:T(1024)}, u32[]{:S(2)}) copy-start(f32[1536]{0:T(1024)} %get-tuple-element.176) | copy-start | bytes 18436
  306.2 8.2 %copy-start.10 = (f32[1536]{0:T(1024)S(1)}, f32[1536]{0:T(1024)}, u32[]{:S(2)}) copy-start(f32[1536]{0:T(1024)} %get-tuple-element.177) | copy-start | bytes 18436
  306.2 8.2 %copy-start.11 = (f32[1536]{0:T(1024)S(1)}, f32[1536]{0:T(1024)}, u32[]{:S(2)}) copy-start(f32[1536]{0:T(1024)} %get-tuple-element.178) | copy-start | bytes 18436
  306.2 8.2 %copy-start.12 = (f32[1536]{0:T(1024)S(1)}, f32[1536]{0:T(1024)}, u32[]{:S(2)}) copy-start(f32[1536]{0:T(1024)} %get-tuple-element.179) | copy-start | bytes 18436
  306.2 8.2 %copy-start.13 = (f32[1536]{0:T(1024)S(1)}, f32[1536]{0:T(1024)}, u32[]{:S(2)}) copy-start(f32[1536]{0:T(1024)} %get-tuple-element.180) | copy-start | bytes 18436
  306.2 8.2 %copy-start.14 = (f32[1536]{0:T(1024)S(1)}, f32[1536]{0:T(1024)}, u32[]{:S(2)}) copy-start(f32[1536]{0:T(1024)} %get-tuple-element.181) | copy-start | bytes 18436
  306.2 8.2 %copy-start.15 = (f32[1536]{0:T(1024)S(1)}, f32[1536]{0:T(1024)}, u32[]{:S(2)}) copy-start(f32[1536]{0:T(1024)} %get-tuple-element.182) | copy-start | bytes 18436
  306.3 8.2 %copy-start.16 = (f32[1536]{0:T(1024)S(1)}, f32[1536]{0:T(1024)}, u32[]{:S(2)}) copy-start(f32[1536]{0:T(1024)} %get-tuple-element.183) | copy-start | bytes 18436
  306.3 8.2 %copy-start.17 = (f32[1536]{0:T(1024)S(1)}, f32[1536]{0:T(1024)}, u32[]{:S(2)}) copy-start(f32[1536]{0:T(1024)} %get-tuple-element.184) | copy-start | bytes 18436
  306.3 8.2 %copy-start.18 = (f32[1536]{0:T(1024)S(1)}, f32[1536]{0:T(1024)}, u32[]{:S(2)}) copy-start(f32[1536]{0:T(1024)} %get-tuple-element.185) | copy-start | bytes 18436
  306.3 8.2 %copy-start.19 = (f32[1536]{0:T(1024)S(1)}, f32[1536]{0:T(1024)}, u32[]{:S(2)}) copy-start(f32[1536]{0:T(1024)} %get-tuple-element.186) | copy-start | bytes 18436
  306.3 8.2 %copy-start.20 = (f32[1536]{0:T(1024)S(1)}, f32[1536]{0:T(1024)}, u32[]{:S(2)}) copy-start(f32[1536]{0:T(1024)} %get-tuple-element.187) | copy-start | bytes 18436
  306.3 8.2 %copy-start.21 = (f32[1536]{0:T(1024)S(1)}, f32[1536]{0:T(1024)}, u32[]{:S(2)}) copy-start(f32[1536]{0:T(1024)} %get-tuple-element.188) | copy-start | bytes 18436
  306.3 8.2 %copy-start.22 = (f32[1536]{0:T(1024)S(1)}, f32[1536]{0:T(1024)}, u32[]{:S(2)}) copy-start(f32[1536]{0:T(1024)} %get-tuple-element.189) | copy-start | bytes 18436
  306.3 8.2 %copy-start.23 = (f32[1536]{0:T(1024)S(1)}, f32[1536]{0:T(1024)}, u32[]{:S(2)}) copy-start(f32[1536]{0:T(1024)} %get-tuple-element.190) | copy-start | bytes 18436
  306.8 3.3 collective-permute-start
  308.1 6.2 %collective-permute-start.1 = (bf16[15,1536]{1,0:T(8,128)(2,1)S(1)}, bf16[15,1536]{1,0:T(8,128)(2,1)S(1)}, u32[]{:S(2)}, u32[]{:S(2)}) collective-permute-start(bf16[15,1536]{1,0:T(8,128)(2,1)S(1)} %get-tuple-element.225), channel_id=1, source_target_pairs={{1,0},{2,1},{3,2},{4,3},{5,4},{6,5},{7,6},{8,7},{9,8},{10,9},{11,1... | collective-permute-start | bytes 138248 | tf_op jit(solution)/shard_map/ppermute | solution.py:24
  409.9 36.2 %all-to-all-start.1 = ((bf16[16,42,1536]{2,1,0:T(8,128)(2,1)}), bf16[16,42,1536]{2,1,0:T(8,128)(2,1)}, u32[]{:S(2)}, u32[]{:S(2)}) async-start(bf16[16,42,1536]{2,1,0:T(8,128)(2,1)} %reshape.195), calls=%async_computation.1 | async-start | bytes 4718592 | tf_op jit(solution)/shard_map/all_to_all | solution.py:146
  (27 other events, 190.1 us)
Sparse Core Ops, SparseCore 0:
  16.3 94.0 all-gather.7
  112.2 88.1 all-gather.9
  202.1 76.1 all-gather.11
  279.9 92.3 all-gather.13
where the time goes:
time: 465 us; the launch traced here: 462 us
  waiting for transfers between devices  188 us (40%)
  matrix products  99.9 us (21%)
  local copies, waits for them, and re-layouts  65.8 us (14%)
  blocking collectives  50.4 us (11%)
  other arithmetic  36.1 us (8%)
  between operations  14.1 us (3%)
  starting transfers between devices  7.7 us (2%)
    all_gather x1, waiting for transfers between devices, body(): piece_values = lax.all_gather(value_rows[0], 'tm', axis=0, tiled=True)  79.9 us
    all_gather x1, waiting for transfers between devices, body(): piece_keys = lax.all_gather(key_unit, 'tm', axis=0, tiled=True)  75.4 us
    all_to_all x1, blocking collectives, body(): lax.all_to_all(outgoing, 'dp', split_axis=0, concat_axis=0, tiled=True)  50.4 us
    dot_general x16, matrix products, per_head(): lax.dot_general(query_one, key_one, (((1,), (1,)), ((), ())), preferred_e...  45.6 us
    dot_general x16, matrix products, per_head(): jnp.dot(weights.astype(jnp.bfloat16), value_one, preferred_element_type=j...  36.1 us
    all_to_all x1, waiting for transfers between devices, body(): lax.all_to_all(produced.astype(jnp.bfloat16).reshape(experts, capacity, D...  26.4 us
    reduce_sum x1, other arithmetic, layer_norm(): average = jnp.mean(values, axis=-1, keepdims=True)  17.4 us
    dot_general x1, matrix products, body(): jnp.dot(hidden_part, piece_out, preferred_element_type=jnp.float32)  14.9 us
  transfers between devices with their start and end apart: 7, of which 5 were waited for; matrix products, arithmetic and copies ran while one was open for 35% of the time, Pallas kernels for 0%

commit v1 on v0

v1 whole, which is shorter than its diff:
```python
import functools

import jax
import jax.numpy as jnp
from jax import lax
from jax.experimental import pallas as pl
from jax.experimental.pallas import tpu as pltpu
from jax.sharding import PartitionSpec as P

D = 1536
HEADS = 16
HEAD_DIM = 64
KERNEL = 31
HALF = 15
TOPK = 2
RECS = 4
EDGE = 16
CAP_PAD = 48
MESH = pl.DeviceIdType.MESH
BF = jnp.bfloat16
F32 = jnp.float32
VMEM_LIMIT = 60 * 1024 * 1024


def any_spec():
    return pl.BlockSpec(memory_space=pl.ANY)


def vmem_spec():
    return pl.BlockSpec(memory_space=pltpu.VMEM)


def smem_spec():
    return pl.BlockSpec(memory_space=pltpu.SMEM)


def dot(a, b, dims=((1,), (0,))):
    return lax.dot_general(a, b, (dims, ((), ())), preferred_element_type=F32)


def greet(axis, count):
    barrier = pltpu.get_barrier_semaphore()
    me = lax.axis_index(axis)
    for step in range(1, count):
        pl.semaphore_signal(
            barrier, inc=1, device_id={axis: lax.rem(me + step, count)}, device_id_type=MESH
        )


def greeted(total):
    pl.semaphore_wait(pltpu.get_barrier_semaphore(), total)


def spread(axis, count, source, target, send_sem, recv_sem, own_sem):
    me = lax.axis_index(axis)
    copies = []
    for step in range(1, count):
        peer = lax.rem(me + step, count)
        copy = pltpu.make_async_remote_copy(
            src_ref=source.at[peer],
            dst_ref=target.at[me],
            send_sem=send_sem.at[step - 1],
            recv_sem=recv_sem.at[step - 1],
            device_id={axis: peer},
            device_id_type=MESH,
        )
        copy.start()
        copies.append(copy)
    own = pltpu.make_async_copy(source.at[me], target.at[me], own_sem)
    own.start()
    copies.append(own)
    return copies


def low_lanes(shape):
    return lax.broadcasted_iota(jnp.int32, shape, 1) < HEAD_DIM


def pair_ones():
    row = lax.broadcasted_iota(jnp.int32, (128, 128), 0) // HEAD_DIM
    col = lax.broadcasted_iota(jnp.int32, (128, 128), 1) // HEAD_DIM
    return (row == col).astype(F32).astype(BF)


def unit_pair(tile, ones):
    square = tile * tile
    high = square.astype(BF)
    rest = (square - high.astype(F32)).astype(BF)
    total = dot(high, ones) + dot(rest, ones)
    return tile * lax.rsqrt(total + 1e-06)


def swap(tile):
    return pltpu.roll(tile, HEAD_DIM, 1)


def heads_kernel(count, q_ref, k_ref, v_ref, out_ref, pack, send_sem, recv_sem, own_sem):
    greet("tm", count)
    rows = q_ref.shape[0]
    part = rows // 2
    ones = pair_ones()
    low = low_lanes((rows, 128))
    low_part = low_lanes((part, 128))
    for pair in range(HEADS // 2):
        lanes = slice(128 * pair, 128 * pair + 128)
        q = unit_pair(q_ref[:, lanes].astype(F32), ones)
        k = unit_pair(k_ref[:, lanes].astype(F32), ones)
        pack[2 * pair, :rows, :] = jnp.where(low, q, swap(k)).astype(BF)
        pack[2 * pair + 1, :rows, :] = jnp.where(low, swap(q), k).astype(BF)
        upper = v_ref[:part, lanes].astype(F32)
        lower = v_ref[part:, lanes].astype(F32)
        pack[2 * pair, rows:, :] = jnp.where(low_part, upper, swap(lower)).astype(BF)
        pack[2 * pair + 1, rows:, :] = jnp.where(low_part, swap(upper), lower).astype(BF)
    greeted(count - 1)
    for copy in spread("tm", count, pack, out_ref, send_sem, recv_sem, own_sem):
        copy.wait()


TQ = 256
TK = 256


def attend_kernel(
    count, scale_ref, lengths_ref, in_ref, out_ref, qs, ks, vs, outs, key_label, own_label
):
    rows = in_ref.shape[1] * 2 // 3
    part = rows // 2
    frames = rows * count
    me = lax.axis_index("tm")
    scale = scale_ref[me] * 1.4426950408889634
    ends = [lengths_ref[0, 0]]
    for r in range(1, RECS):
        ends.append(ends[-1] + lengths_ref[0, r])
    low = low_lanes((rows, 128))
    low_part = low_lanes((part, 128))

    def unpack(block, carry):
        base = pl.multiple_of(block * rows, 32)
        tile = in_ref[block, :rows, :].astype(F32)
        qs[pl.ds(base, rows), :] = jnp.where(low, tile, 0.0).astype(BF)
        ks[pl.ds(base, rows), :] = swap(tile).astype(BF)
        values = in_ref[block, rows:, :].astype(F32)
        vs[pl.ds(base, part), :] = jnp.where(low_part, values, 1.0).astype(BF)
        vs[pl.ds(base + part, part), :] = jnp.where(low_part, swap(values), 1.0).astype(BF)
        return carry

    lax.fori_loop(0, count, unpack, 0)
    spot = lax.broadcasted_iota(jnp.int32, (8, frames), 1)
    key_label[...] = sum((spot >= ends[r]).astype(jnp.int32) for r in range(RECS - 1))
    outs[:EDGE, :] = jnp.zeros((EDGE, 128), BF)
    outs[EDGE + frames :, :] = jnp.zeros((EDGE, 128), BF)

    def one_block(step, carry):
        base = pl.multiple_of(step * TQ, TQ)
        last = base + (TQ - 1)
        first_key = jnp.int32(0)
        for r in range(RECS - 1):
            first_key = jnp.where(base >= ends[r], ends[r], first_key)
        end_key = ends[RECS - 1]
        for r in range(RECS - 2, -1, -1):
            end_key = jnp.where(last < ends[r], ends[r], end_key)
        place = base + lax.broadcasted_iota(jnp.int32, (TQ, 128), 0)
        own = sum((place >= ends[r]).astype(jnp.int32) for r in range(RECS - 1))
        own_label[...] = own
        query = qs[pl.ds(base, TQ), :]

        def one_key(tile, total):
            start = pl.multiple_of(tile * TK, TK)
            scores = dot(query, ks[pl.ds(start, TK), :], ((1,), (1,)))
            powers = jnp.exp2(scores * scale - scale)
            label = jnp.broadcast_to(key_label[0:1, pl.ds(start, TK)], (TQ, TK))
            wide = jnp.concatenate([own_label[...]] * (TK // 128), axis=1)
            weight = jnp.where(wide == label, powers, 0.0).astype(BF)
            return total + dot(weight, vs[pl.ds(start, TK), :])

        total = lax.fori_loop(
            first_key // TK, (end_key + TK - 1) // TK, one_key, jnp.zeros((TQ, 128), F32)
        )
        outs[pl.ds(EDGE + base, TQ), :] = (total / swap(total)).astype(BF)
        return carry

    lax.fori_loop(0, frames // TQ, one_block, 0)
    half = (rows + 2 * EDGE) // 2
    low_half = low_lanes((half, 128))

    def deal(block, carry):
        base = pl.multiple_of(block * rows, 32)
        upper = outs[pl.ds(base, half), :].astype(F32)
        lower = outs[pl.ds(base + half, half), :].astype(F32)
        out_ref[block] = jnp.where(low_half, upper, swap(lower)).astype(BF)
        return carry

    lax.fori_loop(0, count, deal, 0)


def norm_rows(values):
    centered = values - jnp.mean(values, axis=-1, keepdims=True)
    spread_of = jnp.mean(centered * centered, axis=-1, keepdims=True)
    return centered * lax.rsqrt(spread_of + 1e-05)


def slots_of(routes, experts):
    rows = routes.shape[0]
    lane = lax.broadcasted_iota(jnp.int32, (rows, 128), 1)
    hot = [(routes[:, k : k + 1] == lane).astype(F32) for k in range(TOPK)]
    picks = (hot[0] + hot[1]).astype(BF)
    below = lax.broadcasted_iota(jnp.int32, (rows, rows), 1) < lax.broadcasted_iota(
        jnp.int32, (rows, rows), 0
    )
    ranks = dot(below.astype(F32).astype(BF), picks)
    slots = [
        routes[:, k : k + 1] * CAP_PAD
        + jnp.sum(hot[k] * ranks, axis=1, keepdims=True).astype(jnp.int32)
        for k in range(TOPK)
    ]
    places = lax.broadcasted_iota(jnp.int32, (rows, experts * CAP_PAD), 1)
    return hot, [(slot == places).astype(F32).astype(BF) for slot in slots]


def middle_kernel(
    tm,
    dp,
    att_ref,
    proj_ref,
    taps_ref,
    router_ref,
    routes_ref,
    lengths_ref,
    arrived_ref,
    second_ref,
    gates_ref,
    heads,
    first_s,
    normed,
    label,
    outgoing,
    send_a,
    recv_a,
    own_a,
    send_b,
    recv_b,
    own_b,
):
    greet("tm", tm)
    greet("dp", dp)
    rows = routes_ref.shape[0]
    wide = rows + 2 * EDGE
    half = wide // 2
    greeted(tm + dp - 2)
    back = spread("tm", tm, att_ref, heads, send_a, recv_a, own_a)
    place = (
        lax.axis_index("tm") * rows - EDGE + lax.broadcasted_iota(jnp.int32, (wide, 128), 0)
    )
    frames = rows * tm
    mark = jnp.zeros((wide, 128), jnp.int32)
    end = jnp.int32(0)
    for r in range(RECS - 1):
        end = end + lengths_ref[0, r]
        mark = mark + (place >= end).astype(jnp.int32)
    mark = jnp.where(place < 0, -1, jnp.where(place >= frames, RECS, mark))
    label[...] = mark
    for copy in back:
        copy.wait()
    low = low_lanes((half, 128))
    for part in range(2):
        tiles = []
        for pair in range(HEADS // 2):
            a = heads[2 * pair].astype(F32)
            b = heads[2 * pair + 1].astype(F32)
            if part == 0:
                tiles.append(jnp.where(low, a, swap(b)).astype(BF))
            else:
                tiles.append(jnp.where(low, swap(a), b).astype(BF))
        attended = jnp.concatenate(tiles, axis=1)
        first = dot(attended, proj_ref[...])
        first_s[pl.ds(part * half, half), :] = first
        unit = norm_rows(first).astype(BF).astype(F32)
        for column in range(D // 128):
            normed[column, pl.ds(part * half, half), :] = unit[:, column * 128 : column * 128 + 128]

    strip = 256
    group = 32

    def conv_rows(step, carry):
        base = pl.multiple_of(step * group, group)
        own = label[pl.ds(base + EDGE, group), :]
        for column in range(D // strip):
            total = [jnp.zeros((group, 128), F32)] * (strip // 128)
            for tap in range(KERNEL):
                shift = tap + EDGE - HALF
                same = label[pl.ds(base + shift, group), :] == own
                for n in range(strip // 128):
                    lanes = slice(column * strip + 128 * n, column * strip + 128 * n + 128)
                    value = normed[column * (strip // 128) + n, pl.ds(base + shift, group), :]
                    total[n] = total[n] + jnp.where(same, value * taps_ref[tap : tap + 1, lanes], 0.0)
            for n in range(strip // 128):
                lanes = slice(column * strip + 128 * n, column * strip + 128 * n + 128)
                second_ref[pl.ds(base, group), lanes] = first_s[
                    pl.ds(base + EDGE, group), lanes
                ] + total[n] / (1.0 + jnp.exp(-total[n]))
        return carry

    lax.fori_loop(0, rows // group, conv_rows, 0)
    mixed = norm_rows(second_ref[...]).astype(BF)
    logits = dot(mixed, router_ref[...])
    hot, places = slots_of(routes_ref[...], dp)
    powers = jnp.exp(logits)
    chosen = [jnp.sum(hot[k] * powers, axis=1, keepdims=True) for k in range(TOPK)]
    whole = chosen[0] + chosen[1]
    lane = lax.broadcasted_iota(jnp.int32, (rows, 128), 1)
    gates_ref[...] = jnp.where(lane == 0, chosen[0] / whole, chosen[1] / whole)
    both = places[0] + places[1]
    for expert in range(dp):
        cut = both[:, expert * CAP_PAD : (expert + 1) * CAP_PAD]
        outgoing[expert] = dot(cut, mixed, ((0,), (0,))).astype(BF)
    for copy in spread("dp", dp, outgoing, arrived_ref, send_b, recv_b, own_b):
        copy.wait()


def experts_kernel(
    dp,
    arrived_ref,
    in_ref,
    out_w_ref,
    routes_ref,
    second_ref,
    gates_ref,
    out_ref,
    hidden,
    produced,
    returned,
    send_sem,
    recv_sem,
    own_sem,
):
    greet("dp", dp)
    rows = routes_ref.shape[0]
    units = in_ref.shape[0]
    count = dp * CAP_PAD
    piece = 512
    for column in range(units // piece):
        cut = slice(column * piece, (column + 1) * piece)
        tokens = arrived_ref[...].reshape(count, D)
        value = dot(tokens, in_ref[cut, :], ((1,), (1,)))
        hidden[:, cut] = (value / (1.0 + jnp.exp(-value))).astype(BF)
    for column in range(D // piece):
        cut = slice(column * piece, (column + 1) * piece)
        value = dot(hidden[...], out_w_ref[:, cut]).astype(BF)
        produced[:, :, cut] = value.reshape(dp, CAP_PAD, piece)
    greeted(dp - 1)
    copies = spread("dp", dp, produced, returned, send_sem, recv_sem, own_sem)
    _, places = slots_of(routes_ref[...], dp)
    for copy in copies:
        copy.wait()
    for column in range(D // piece):
        cut = slice(column * piece, (column + 1) * piece)
        results = returned[:, :, cut].reshape(count, piece)
        mixture = gates_ref[:, 0:1] * dot(places[0], results)
        mixture = mixture + gates_ref[:, 1:2] * dot(places[1], results)
        out_ref[:, cut] = (second_ref[:, cut] + 0.5 * mixture).astype(BF)


def params(collective_id=None):
    if collective_id is None:
        return pltpu.CompilerParams(vmem_limit_bytes=VMEM_LIMIT)
    return pltpu.CompilerParams(
        vmem_limit_bytes=VMEM_LIMIT, collective_id=collective_id, has_side_effects=True
    )


def exchange_sems(count):
    return [
        pltpu.SemaphoreType.DMA((count - 1,)),
        pltpu.SemaphoreType.DMA((count - 1,)),
        pltpu.SemaphoreType.DMA,
    ]


def body(
    query_rows,
    key_rows,
    value_rows,
    head_scale,
    out_proj,
    conv_taps,
    router,
    expert_in,
    expert_out,
    lengths,
    routes,
):
    rows = query_rows.shape[1]
    tm = lax.axis_size("tm")
    dp = lax.axis_size("dp")
    frames = rows * tm
    wide = rows + 2 * EDGE
    stacked = rows + rows // 2
    piece_in = lax.all_gather(expert_in[0], "tm", axis=0, tiled=True)
    piece_out = lax.all_gather(expert_out[0], "tm", axis=0, tiled=True)
    units = piece_in.shape[0]
    packed = pl.pallas_call(
        functools.partial(heads_kernel, tm),
        out_shape=jax.ShapeDtypeStruct((tm, stacked, 128), BF),
        in_specs=[vmem_spec()] * 3,
        out_specs=any_spec(),
        scratch_shapes=[pltpu.VMEM((tm, stacked, 128), BF)] + exchange_sems(tm),
        compiler_params=params(0),
        name="heads",
    )(query_rows[0], key_rows[0], value_rows[0])
    attended = pl.pallas_call(
        functools.partial(attend_kernel, tm),
        out_shape=jax.ShapeDtypeStruct((tm, wide // 2, 128), BF),
        in_specs=[smem_spec(), smem_spec(), vmem_spec()],
        out_specs=vmem_spec(),
        scratch_shapes=[
            pltpu.VMEM((frames, 128), BF),
            pltpu.VMEM((frames, 128), BF),
            pltpu.VMEM((frames, 128), BF),
            pltpu.VMEM((frames + 2 * EDGE, 128), BF),
            pltpu.VMEM((8, frames), jnp.int32),
            pltpu.VMEM((TQ, 128), jnp.int32),
        ],
        compiler_params=params(),
        name="attend",
    )(head_scale, lengths, packed)
    wide_router = jnp.pad(router, ((0, 0), (0, 128 - router.shape[1])))
    arrived, second, gates = pl.pallas_call(
        functools.partial(middle_kernel, tm, dp),
        out_shape=(
            jax.ShapeDtypeStruct((dp, CAP_PAD, D), BF),
            jax.ShapeDtypeStruct((rows, D), F32),
            jax.ShapeDtypeStruct((rows, 128), F32),
        ),
        in_specs=[any_spec()] + [vmem_spec()] * 4 + [smem_spec()],
        out_specs=(any_spec(), vmem_spec(), vmem_spec()),
        scratch_shapes=[
            pltpu.VMEM((tm, wide // 2, 128), BF),
            pltpu.VMEM((wide, D), F32),
            pltpu.VMEM((D // 128, wide, 128), F32),
            pltpu.VMEM((wide, 128), jnp.int32),
            pltpu.VMEM((dp, CAP_PAD, D), BF),
        ]
        + exchange_sems(tm)
        + exchange_sems(dp),
        compiler_params=params(1),
        name="middle",
    )(attended, out_proj, conv_taps, wide_router, routes[0], lengths)
    out = pl.pallas_call(
        functools.partial(experts_kernel, dp),
        out_shape=jax.ShapeDtypeStruct((rows, D), BF),
        in_specs=[vmem_spec()] * 6,
        out_specs=vmem_spec(),
        scratch_shapes=[
            pltpu.VMEM((dp * CAP_PAD, units), BF),
            pltpu.VMEM((dp, CAP_PAD, D), BF),
            pltpu.VMEM((dp, CAP_PAD, D), BF),
        ]
        + exchange_sems(dp),
        compiler_params=params(2),
        name="experts",
    )(arrived, piece_in, piece_out, routes[0], second, gates)
    return out[None]


def solution(mesh):
    return jax.shard_map(
        body,
        mesh=mesh,
        in_specs=(
            P("dp", "tm", None),
            P("dp", "tm", None),
            P("dp", "tm", None),
            P(),
            P(),
            P(),
            P(),
            P("dp", "tm", None),
            P("dp", "tm", None),
            P("dp", None),
            P("dp", "tm", None),
        ),
        out_specs=P("dp", "tm", None),
        check_vma=False,
    )
```

time: 465 us -> 299 us (0.64)
  Pallas kernels: 0 us -> 273 us
  waiting for transfers between devices: 188 us -> 1.45 us
  matrix products: 99.9 us -> 0 us
  local copies, waits for them, and re-layouts: 65.8 us -> 5.31 us
  blocking collectives: 50.4 us -> 0 us
  other arithmetic: 36.1 us -> 0 us
  starting transfers between devices: 7.7 us -> 0.04 us
    pallas_call x0 -> x4, Pallas kernels: none -> 273 us  [the longest x1 117 us: body(): pl.pallas_call(functools.partial(middle_kernel, tm, dp), out_shape=(jax.S...]
    all_gather x2 -> x0, waiting for transfers between devices: 155 us -> none  [the longest x1 79.9 us: body(): piece_values = lax.all_gather(value_rows[0], 'tm', axis=0, tiled=True)]
    dot_general x36 -> x0, matrix products: 99.9 us -> none  [the longest x16 45.6 us: per_head(): lax.dot_general(query_one, key_one, (((1,), (1,)), ((), ())), preferred_e...]
    all_to_all x1 -> x0, blocking collectives: 50.4 us -> none  [body(): lax.all_to_all(outgoing, 'dp', split_axis=0, concat_axis=0, tiled=True)]
    all_to_all x1 -> x0, waiting for transfers between devices: 26.4 us -> none  [body(): lax.all_to_all(produced.astype(jnp.bfloat16).reshape(experts, capacity, D...]
    reduce_sum x11 -> x0, other arithmetic: 21.6 us -> none  [the longest x1 17.4 us: layer_norm(): average = jnp.mean(values, axis=-1, keepdims=True)]
    all_gather x2 -> x0, local copies, waits for them, and re-layouts: 20.1 us -> none  [the longest x1 10.1 us: body(): piece_values = lax.all_gather(value_rows[0], 'tm', axis=0, tiled=True)]
    reshape x4 -> x0, local copies, waits for them, and re-layouts: 11.9 us -> none  [the longest x1 4.04 us: body(): produced.astype(jnp.bfloat16).reshape(experts, capacity, D)]
  transfers between devices with their start and end apart: 7 -> 2, of which waited for: 5 -> 0; matrix products, arithmetic and copies ran while one was open for 35% -> 1% of each run, Pallas kernels for 0% -> 76%
where the time goes in v1:
time: 299 us; the launch traced here: 294 us
  Pallas kernels  273 us (91%)
  between operations  13.4 us (4%)
  local copies, waits for them, and re-layouts  5.31 us (2%)
    pallas_call x1, Pallas kernels, body(): pl.pallas_call(functools.partial(middle_kernel, tm, dp), out_shape=(jax.S...  117 us
    pallas_call x1, Pallas kernels, body(): pl.pallas_call(functools.partial(heads_kernel, tm), out_shape=jax.ShapeDt...  54.5 us
    pallas_call x1, Pallas kernels, body(): pl.pallas_call(functools.partial(attend_kernel, tm), out_shape=jax.ShapeD...  52.8 us
    pallas_call x1, Pallas kernels, body(): pl.pallas_call(functools.partial(experts_kernel, dp), out_shape=jax.Shape...  49.1 us
  transfers between devices with their start and end apart: 2, of which 0 were waited for; matrix products, arithmetic and copies ran while one was open for 1% of the time, Pallas kernels for 76%

profile of v1, /device:TPU:1, one launch (start us, length us, event | category | flops | bytes accessed | tf_op | source)
XLA Modules:
  0.0 293.7 jit_solution(2416869378927369987)
XLA Ops:
  6.5 0.0 all-gather.5.cloned.1.call-start
  6.5 0.7 all-gather.5.cloned.1.call-update
  7.3 0.0 all-gather.7.cloned.1.call-start
  7.3 0.7 all-gather.7.cloned.1.call-update
  8.0 1.4 copy.13
  9.5 1.0 copy.12
  10.5 0.9 pad.4.router_ref
  11.3 54.5 %heads.1.in_ref = bf16[16,336,128]{2,1,0:T(8,128)(2,1)} custom-call(bf16[224,1024]{1,0:T(8,128)(2,1)} %bitcast.12, bf16[224,1024]{1,0:T(8,128)(2,1)} %bitcast.13, bf16[224,1024]{1,0:T(8,128)(2,1)} %bitcast.14), custom_call_target="tpu_custom_call" | custom-call | tf_op jit(solution)/shard_map/heads/pallas_call | solution.py:401
  65.8 52.8 %attend.1.att_ref = bf16[16,128,128]{2,1,0:T(8,128)(2,1)} custom-call(f32[16]{0:T(128)} %scale_ref.1, s32[1,4]{1,0:T(1,128)} %lengths_ref.3, bf16[16,336,128]{2,1,0:T(8,128)(2,1)} %heads.1.in_ref), custom_call_target="tpu_custom_call" | custom-call | tf_op jit(solution)/shard_map/attend/pallas_call | solution.py:410
  118.6 117.1 %middle.1 = (bf16[16,48,1536]{2,1,0:T(8,128)(2,1)}, f32[224,1536]{1,0:T(8,128)}, f32[224,128]{1,0:T(8,128)}) custom-call(bf16[16,128,128]{2,1,0:T(8,128)(2,1)} %attend.1.att_ref, bf16[1024,1536]{1,0:T(8,128)(2,1)} %proj_ref.1, f32[31,1536]{1,0:T(8,128)} %taps_ref.1, bf16[1536,128]{1,0:T(8,128)(2,1)} %pad.4.router_ref, s32[224,2]{1,0:T(8,128)} %bitcast.10, ...), custom_call_target="tpu_custom_call" | custom-call | tf_op jit(solution)/shard_map/middle/pallas_call | solution.py:427
  235.7 0.0 all-gather.5.cloned.1.call-done
  235.7 0.0 all-gather.7.cloned.1.call-done
  235.8 49.1 %experts.1 = bf16[224,1536]{1,0:T(8,128)(2,1)} custom-call(bf16[16,48,1536]{2,1,0:T(8,128)(2,1)} %get-tuple-element.8.arrived_ref, bf16[2048,1536]{1,0:T(8,128)(2,1)} %bitcast.7, bf16[2048,1536]{1,0:T(8,128)(2,1)} %bitcast.8, s32[224,2]{1,0:T(8,128)} %bitcast.11, f32[224,1536]{1,0:T(8,128)} %get-tuple-element.9.second_ref, ...), custom_call_target="tpu_custom_call" | custom-call | tf_op jit(solution)/shard_map/experts/pallas_call | solution.py:448
  284.8 2.0 copy.15
Async XLA Ops:
  6.5 229.2 %all-gather.5.cloned.1.call-start = ((), (), s32[]{:S(2)}) async-start(), calls=%async_computation | async-start | bytes 6684672 | tf_op jit(solution)/shard_map/all_gather | solution.py:398
  7.3 228.5 %all-gather.7.cloned.1.call-start = ((), (), s32[]{:S(2)}) async-start(), calls=%async_computation.1 | async-start | bytes 6684672 | tf_op jit(solution)/shard_map/all_gather | solution.py:399
Sparse Core Ops, SparseCore 0:
  9.1 106.0 all-gather.4
  117.0 108.2 all-gather.6

commit v2 on v1

v2 whole, which is shorter than its diff:
```python
import functools

import jax
import jax.numpy as jnp
from jax import lax
from jax.experimental import pallas as pl
from jax.experimental.pallas import tpu as pltpu
from jax.sharding import PartitionSpec as P

D = 1536
HEADS = 16
HEAD_DIM = 64
KERNEL = 31
HALF = 15
TOPK = 2
RECS = 4
EDGE = 16
CAP_PAD = 48
MESH = pl.DeviceIdType.MESH
BF = jnp.bfloat16
F32 = jnp.float32
VMEM_LIMIT = 60 * 1024 * 1024


def any_spec():
    return pl.BlockSpec(memory_space=pl.ANY)


def vmem_spec():
    return pl.BlockSpec(memory_space=pltpu.VMEM)


def smem_spec():
    return pl.BlockSpec(memory_space=pltpu.SMEM)


def dot(a, b, dims=((1,), (0,))):
    return lax.dot_general(a, b, (dims, ((), ())), preferred_element_type=F32)


def greet(axis, count):
    barrier = pltpu.get_barrier_semaphore()
    me = lax.axis_index(axis)
    for step in range(1, count):
        pl.semaphore_signal(
            barrier, inc=1, device_id={axis: lax.rem(me + step, count)}, device_id_type=MESH
        )


def greeted(total):
    pl.semaphore_wait(pltpu.get_barrier_semaphore(), total)


def spread(axis, count, source, target, send_sem, recv_sem, own_sem):
    me = lax.axis_index(axis)
    copies = []
    for step in range(1, count):
        peer = lax.rem(me + step, count)
        copy = pltpu.make_async_remote_copy(
            src_ref=source.at[peer],
            dst_ref=target.at[me],
            send_sem=send_sem.at[step - 1],
            recv_sem=recv_sem.at[step - 1],
            device_id={axis: peer},
            device_id_type=MESH,
        )
        copy.start()
        copies.append(copy)
    own = pltpu.make_async_copy(source.at[me], target.at[me], own_sem)
    own.start()
    copies.append(own)
    return copies


def low_lanes(shape):
    return lax.broadcasted_iota(jnp.int32, shape, 1) < HEAD_DIM


def pair_ones():
    row = lax.broadcasted_iota(jnp.int32, (128, 128), 0) // HEAD_DIM
    col = lax.broadcasted_iota(jnp.int32, (128, 128), 1) // HEAD_DIM
    return (row == col).astype(F32).astype(BF)


def unit_pair(tile, ones):
    square = tile * tile
    high = square.astype(BF)
    rest = (square - high.astype(F32)).astype(BF)
    total = dot(high, ones) + dot(rest, ones)
    return tile * lax.rsqrt(total + 1e-06)


def swap(tile):
    return pltpu.roll(tile, HEAD_DIM, 1)


def norm_rows(values):
    centered = values - jnp.mean(values, axis=-1, keepdims=True)
    spread_of = jnp.mean(centered * centered, axis=-1, keepdims=True)
    return centered * lax.rsqrt(spread_of + 1e-05)


def slots_of(routes, experts):
    rows = routes.shape[0]
    lane = lax.broadcasted_iota(jnp.int32, (rows, 128), 1)
    hot = [(routes[:, k : k + 1] == lane).astype(F32) for k in range(TOPK)]
    picks = (hot[0] + hot[1]).astype(BF)
    below = lax.broadcasted_iota(jnp.int32, (rows, rows), 1) < lax.broadcasted_iota(
        jnp.int32, (rows, rows), 0
    )
    ranks = dot(below.astype(F32).astype(BF), picks)
    slots = [
        routes[:, k : k + 1] * CAP_PAD
        + jnp.sum(hot[k] * ranks, axis=1, keepdims=True).astype(jnp.int32)
        for k in range(TOPK)
    ]
    places = lax.broadcasted_iota(jnp.int32, (rows, experts * CAP_PAD), 1)
    return hot, [(slot == places).astype(F32).astype(BF) for slot in slots]


GATHER_IDS = 30
HOPS = 4


class Gather:
    def __init__(self, w_in, w_out, send_sem, recv_sem):
        self.w_in, self.w_out = w_in, w_out
        self.send_sem, self.recv_sem = send_sem, recv_sem
        self.me = lax.axis_index("tm")
        self.own = self.me // 8 * 8
        self.other = 8 - self.own
        self.z = self.me - self.own

    def at(self, base, shift):
        return base + lax.rem(self.z + shift + 8, 8)

    def table(self):
        w_in, w_out, own, other, at = self.w_in, self.w_out, self.own, self.other, self.at
        up, down, across = at(own, 1), at(own, -1), at(other, 0)
        table = {0: (w_in, self.me, across, across), 1: (w_out, self.me, across, across)}
        for h in range(1, HOPS + 1):
            table[1 + h] = (w_out, at(own, -h), across, at(other, -h))
            table[8 + h] = (w_out, at(own, 1 - h), up, at(own, -h))
            table[15 + h] = (w_in, at(own, 1 - h), up, at(own, -h))
            table[25 + h] = (w_in, at(other, h - 1), down, at(other, h))
        for h in range(1, HOPS):
            table[5 + h] = (w_out, at(own, h), across, at(other, h))
            table[12 + h] = (w_out, at(own, h - 1), down, at(own, h))
            table[19 + h] = (w_in, at(other, 1 - h), up, at(other, -h))
            table[22 + h] = (w_in, at(own, h - 1), down, at(own, h))
        return table

    def copy(self, n, chunk):
        buffer, _, peer, _ = self.table()[n]
        return pltpu.make_async_remote_copy(
            src_ref=buffer.at[chunk],
            dst_ref=buffer.at[chunk],
            send_sem=self.send_sem.at[n],
            recv_sem=self.recv_sem.at[n],
            device_id={"tm": peer},
            device_id_type=MESH,
        )

    def start(self, *ids):
        for n in ids:
            self.copy(n, self.table()[n][1]).start()

    def receive(self, *ids):
        for n in ids:
            self.copy(n, self.table()[n][3]).wait_recv()

    def finish(self):
        for n in range(GATHER_IDS):
            self.copy(n, self.table()[n][1]).wait_send()

    def event(self, n):
        if n == 0:
            self.start(0, 1, 9, 13)
        elif n == 1:
            self.receive(0)
            self.start(16, 23, 20, 26)
        elif n == 2:
            self.receive(9, 13)
            self.start(10, 14, 2, 6)
        elif n == 3:
            self.receive(16, 23, 20, 26)
            self.start(17, 24, 21, 27)
        elif n == 4:
            self.receive(10, 14)
            self.start(11, 15, 3, 7)
        elif n == 5:
            self.receive(17, 24, 21, 27)
            self.start(18, 25, 22, 28)
        elif n == 6:
            self.receive(11, 15)
            self.start(12, 4, 8)
        elif n == 7:
            self.receive(18, 25, 22, 28)
            self.start(19, 29)
        elif n == 8:
            self.receive(12)
            self.start(5)
        elif n == 9:
            self.receive(19, 29)
        else:
            self.receive(1, 2, 3, 4, 5, 6, 7, 8)


def block_kernel(
    tm,
    dp,
    scale_ref,
    lengths_ref,
    q_ref,
    k_ref,
    v_ref,
    proj_ref,
    taps_ref,
    router_ref,
    routes_ref,
    in_ref,
    out_w_ref,
    out_ref,
    pack,
    held,
    qs,
    ks,
    vs,
    outs,
    att,
    heads,
    first_s,
    normed,
    label,
    second,
    outgoing,
    arrived,
    w_in,
    w_out,
    hidden,
    produced,
    returned,
    gather_send,
    gather_recv,
    load_sem,
    send_h,
    recv_h,
    own_h,
    send_a,
    recv_a,
    send_b,
    recv_b,
    own_b,
    send_c,
    recv_c,
):
    greet("tm", tm)
    greet("dp", dp)
    me = lax.axis_index("tm")
    me_dp = lax.axis_index("dp")
    rows = q_ref.shape[0]
    frames = rows * tm
    part = rows // 2
    wide = rows + 2 * EDGE
    half = wide // 2
    gather = Gather(w_in, w_out, gather_send, gather_recv)
    loads = [
        pltpu.make_async_copy(in_ref.at[0], w_in.at[me], load_sem.at[0]),
        pltpu.make_async_copy(out_w_ref.at[0], w_out.at[me], load_sem.at[1]),
    ]
    for load in loads:
        load.start()
    for load in loads:
        load.wait()
    greeted(tm + dp - 2)
    gather.event(0)

    ones = pair_ones()
    low = low_lanes((rows, 128))
    low_part = low_lanes((part, 128))
    low_half = low_lanes((half, 128))
    for pair in range(HEADS // 2):
        lanes = slice(128 * pair, 128 * pair + 128)
        q = unit_pair(q_ref[:, lanes].astype(F32), ones)
        k = unit_pair(k_ref[:, lanes].astype(F32), ones)
        pack[2 * pair, :rows, :] = jnp.where(low, q, swap(k)).astype(BF)
        pack[2 * pair + 1, :rows, :] = jnp.where(low, swap(q), k).astype(BF)
        upper = v_ref[:part, lanes].astype(F32)
        lower = v_ref[part:, lanes].astype(F32)
        pack[2 * pair, rows:, :] = jnp.where(low_part, upper, swap(lower)).astype(BF)
        pack[2 * pair + 1, rows:, :] = jnp.where(low_part, swap(upper), lower).astype(BF)
    exchange = spread("tm", tm, pack, held, send_h, recv_h, own_h)
    for copy in exchange:
        copy.wait()
    gather.event(1)

    scale = scale_ref[me] * 1.4426950408889634
    ends = []
    for r in range(RECS - 1):
        ends.append(lengths_ref[0, r] + (ends[-1] if ends else 0))
    lane = lax.broadcasted_iota(jnp.int32, (rows, 128), 1)
    minus = lane == HEAD_DIM + RECS

    def unpack(block, carry):
        base = pl.multiple_of(block * rows, 32)
        tile = held[block, :rows, :].astype(F32)
        spot = base + lax.broadcasted_iota(jnp.int32, (rows, 128), 0)
        mark = sum((spot >= end).astype(jnp.int32) for end in ends)
        hit = lane == HEAD_DIM + mark
        apart = jnp.where(hit | (lane > HEAD_DIM + RECS), 0.0, -128.0)
        qs[pl.ds(base, rows), :] = jnp.where(low, tile, jnp.where(minus, -1.0, apart)).astype(BF)
        ks[pl.ds(base, rows), :] = jnp.where(
            low, swap(tile), jnp.where(minus | hit, 1.0, 0.0)
        ).astype(BF)
        values = held[block, rows:, :].astype(F32)
        vs[pl.ds(base, part), :] = jnp.where(low_part, values, 1.0).astype(BF)
        vs[pl.ds(base + part, part), :] = jnp.where(low_part, swap(values), 1.0).astype(BF)
        return carry

    lax.fori_loop(0, tm, unpack, 0)
    outs[:EDGE, :] = jnp.zeros((EDGE, 128), BF)
    outs[EDGE + frames :, :] = jnp.zeros((EDGE, 128), BF)

    def deal(block):
        base = pl.multiple_of(block * rows, 32)
        upper = outs[pl.ds(base, half), :].astype(F32)
        lower = outs[pl.ds(base + half, half), :].astype(F32)
        return jnp.where(low_half, upper, swap(lower)).astype(BF)

    def back(distance):
        peer = lax.rem(me + distance, tm)
        return pltpu.make_async_remote_copy(
            src_ref=att.at[peer],
            dst_ref=heads.at[me],
            send_sem=send_a.at[distance - 1],
            recv_sem=recv_a.at[distance - 1],
            device_id={"tm": peer},
            device_id_type=MESH,
        )

    def attend(step, carry):
        base = pl.multiple_of(lax.rem(me + 1 + step, tm) * rows, 32)
        scores = dot(qs[pl.ds(base, rows), :], ks[...], ((1,), (1,)))
        total = dot(jnp.exp2(scores * scale).astype(BF), vs[...])
        outs[pl.ds(EDGE + base, rows), :] = (total / swap(total)).astype(BF)

        @pl.when(step >= 2)
        def _():
            peer = lax.rem(me + step, tm)
            att[peer] = deal(peer)
            back(step).start()

        @pl.when(step == 1)
        def _():
            gather.event(2)

        @pl.when(step == 13)
        def _():
            gather.event(3)

        return carry

    lax.fori_loop(0, tm, attend, 0)
    att[lax.rem(me + 1, tm)] = deal(lax.rem(me + 1, tm))
    back(1).start()
    heads[me] = deal(me)
    place = me * rows - EDGE + lax.broadcasted_iota(jnp.int32, (wide, 128), 0)
    mark = sum((place >= end).astype(jnp.int32) for end in ends)
    label[...] = jnp.where(place < 0, -1, jnp.where(place >= frames, RECS, mark))
    for distance in range(1, tm):
        back(distance).wait()
    gather.event(4)

    for top in range(2):
        tiles = []
        for pair in range(HEADS // 2):
            a = heads[2 * pair].astype(F32)
            b = heads[2 * pair + 1].astype(F32)
            if top == 0:
                tiles.append(jnp.where(low_half, a, swap(b)).astype(BF))
            else:
                tiles.append(jnp.where(low_half, swap(a), b).astype(BF))
        first = dot(jnp.concatenate(tiles, axis=1), proj_ref[...])
        first_s[pl.ds(top * half, half), :] = first
        unit = norm_rows(first).astype(BF).astype(F32)
        for column in range(D // 128):
            normed[column, pl.ds(top * half, half), :] = unit[:, column * 128 : column * 128 + 128]

    strip = 256
    group = 32

    def conv_rows(step, carry):
        base = pl.multiple_of(step * group, group)
        own = label[pl.ds(base + EDGE, group), :]
        for column in range(D // strip):
            total = [jnp.zeros((group, 128), F32)] * (strip // 128)
            for tap in range(KERNEL):
                shift = tap + EDGE - HALF
                same = label[pl.ds(base + shift, group), :] == own
                for n in range(strip // 128):
                    lanes = slice(column * strip + 128 * n, column * strip + 128 * n + 128)
                    value = normed[column * (strip // 128) + n, pl.ds(base + shift, group), :]
                    total[n] = total[n] + jnp.where(same, value * taps_ref[tap : tap + 1, lanes], 0.0)
            for n in range(strip // 128):
                lanes = slice(column * strip + 128 * n, column * strip + 128 * n + 128)
                second[pl.ds(base, group), lanes] = first_s[
                    pl.ds(base + EDGE, group), lanes
                ] + total[n] / (1.0 + jnp.exp(-total[n]))

        @pl.when(step == 5)
        def _():
            gather.event(5)

        return carry

    lax.fori_loop(0, rows // group, conv_rows, 0)

    mixed = norm_rows(second[...]).astype(BF)
    logits = dot(mixed, router_ref[...])
    hot, places = slots_of(routes_ref[...], dp)
    powers = jnp.exp(logits)
    chosen = [jnp.sum(hot[k] * powers, axis=1, keepdims=True) for k in range(TOPK)]
    whole = chosen[0] + chosen[1]
    gates = [chosen[k] / whole for k in range(TOPK)]
    both = places[0] + places[1]
    for expert in range(dp):
        cut = both[:, expert * CAP_PAD : (expert + 1) * CAP_PAD]
        outgoing[expert] = dot(cut, mixed, ((0,), (0,))).astype(BF)
    dispatch = spread("dp", dp, outgoing, arrived, send_b, recv_b, own_b)
    for n in range(6, 10):
        gather.event(n)
    for copy in dispatch:
        copy.wait()

    units = w_in.shape[0] * w_in.shape[1]
    chunk = w_in.shape[1]
    count = dp * CAP_PAD
    step_chunks = 4
    for column in range(tm // step_chunks):
        cut = slice(column * step_chunks * chunk, (column + 1) * step_chunks * chunk)
        weights = w_in[column * step_chunks : (column + 1) * step_chunks].reshape(-1, D)
        value = dot(arrived[...].reshape(count, D), weights, ((1,), (1,)))
        hidden[:, cut] = (value / (1.0 + jnp.exp(-value))).astype(BF)
    gather.event(10)
    piece = 512
    team = 4
    results = []
    for turn in range(dp // team):
        base = lax.rem(me_dp // team + 1 + turn, dp // team) * team
        start = pl.multiple_of(base * CAP_PAD, team * CAP_PAD)
        for column in range(D // piece):
            cut = slice(column * piece, (column + 1) * piece)
            weights = w_out[:, :, cut].reshape(units, piece)
            value = dot(hidden[pl.ds(start, team * CAP_PAD), :], weights).astype(BF)
            produced[pl.ds(base, team), :, cut] = value.reshape(team, CAP_PAD, piece)
        for n in range(team):
            if turn == dp // team - 1 and n == 0:
                continue
            peer = base + lax.rem(lax.rem(me_dp, team) + n, team)
            distance = lax.rem(peer - me_dp + dp, dp)
            copy = pltpu.make_async_remote_copy(
                src_ref=produced.at[peer],
                dst_ref=returned.at[me_dp],
                send_sem=send_c.at[distance - 1],
                recv_sem=recv_c.at[distance - 1],
                device_id={"dp": peer},
                device_id_type=MESH,
            )
            copy.start()
            results.append(copy)
    returned[me_dp] = produced[me_dp]
    gather.finish()
    for copy in results:
        copy.wait()
    for column in range(D // piece):
        cut = slice(column * piece, (column + 1) * piece)
        value = returned[:, :, cut].reshape(count, piece)
        mixture = gates[0] * dot(places[0], value) + gates[1] * dot(places[1], value)
        out_ref[:, cut] = (second[:, cut] + 0.5 * mixture).astype(BF)


def sems(count):
    return [pltpu.SemaphoreType.DMA((count,))] * 2


def body(
    query_rows,
    key_rows,
    value_rows,
    head_scale,
    out_proj,
    conv_taps,
    router,
    expert_in,
    expert_out,
    lengths,
    routes,
):
    rows = query_rows.shape[1]
    tm = lax.axis_size("tm")
    dp = lax.axis_size("dp")
    frames = rows * tm
    wide = rows + 2 * EDGE
    stacked = rows + rows // 2
    chunk = expert_in.shape[1]
    wide_router = jnp.pad(router, ((0, 0), (0, 128 - router.shape[1])))
    bf = lambda *shape: pltpu.VMEM(shape, BF)
    out = pl.pallas_call(
        functools.partial(block_kernel, tm, dp),
        out_shape=jax.ShapeDtypeStruct((rows, D), BF),
        in_specs=[smem_spec()] * 2 + [vmem_spec()] * 7 + [any_spec()] * 2,
        out_specs=vmem_spec(),
        scratch_shapes=[
            bf(tm, stacked, 128),
            bf(tm, stacked, 128),
            bf(frames, 128),
            bf(frames, 128),
            bf(frames, 128),
            bf(frames + 2 * EDGE, 128),
            bf(tm, wide // 2, 128),
            bf(tm, wide // 2, 128),
            pltpu.VMEM((wide, D), F32),
            pltpu.VMEM((D // 128, wide, 128), F32),
            pltpu.VMEM((wide, 128), jnp.int32),
            pltpu.VMEM((rows, D), F32),
            bf(dp, CAP_PAD, D),
            bf(dp, CAP_PAD, D),
            bf(tm, chunk, D),
            bf(tm, chunk, D),
            bf(dp * CAP_PAD, tm * chunk),
            bf(dp, CAP_PAD, D),
            bf(dp, CAP_PAD, D),
        ]
        + sems(GATHER_IDS)
        + [pltpu.SemaphoreType.DMA((2,))]
        + sems(tm - 1)
        + [pltpu.SemaphoreType.DMA]
        + sems(tm - 1)
        + sems(dp - 1)
        + [pltpu.SemaphoreType.DMA]
        + sems(dp - 1),
        compiler_params=pltpu.CompilerParams(
            vmem_limit_bytes=VMEM_LIMIT, collective_id=0, has_side_effects=True
        ),
        name="block",
    )(
        head_scale,
        lengths,
        query_rows[0],
        key_rows[0],
        value_rows[0],
        out_proj,
        conv_taps,
        wide_router,
        routes[0],
        expert_in,
        expert_out,
    )
    return out[None]


def solution(mesh):
    return jax.shard_map(
        body,
        mesh=mesh,
        in_specs=(
            P("dp", "tm", None),
            P("dp", "tm", None),
            P("dp", "tm", None),
            P(),
            P(),
            P(),
            P(),
            P("dp", "tm", None),
            P("dp", "tm", None),
            P("dp", None),
            P("dp", "tm", None),
        ),
        out_specs=P("dp", "tm", None),
        check_vma=False,
    )
```

time: 299 us -> 228 us (0.76)
  the two profiles are of different devices: /device:TPU:1 before, /device:TPU:49 now
where the time goes in v2:
time: 228 us
  Pallas kernels  222 us (97%)
  local copies, waits for them, and re-layouts  5.29 us (2%)
    pallas_call x1, Pallas kernels, body(): pl.pallas_call(functools.partial(block_kernel, tm, dp), out_shape=jax.Sha...  222 us

profile of v2, /device:TPU:49, one launch (start us, length us, event | category | flops | bytes accessed | tf_op | source)
XLA Modules:
  0.0 227.6 jit_solution(12762492198027622231)
XLA Ops:
  0.0 1.5 copy.13
  1.5 1.0 copy.12
  2.5 0.8 pad.4.router_ref
  3.3 222.3 %block.1 = bf16[224,1536]{1,0:T(8,128)(2,1)} custom-call(f32[16]{0:T(128)} %scale_ref.1, s32[1,4]{1,0:T(1,128)} %lengths_ref.1, bf16[224,1024]{1,0:T(8,128)(2,1)} %bitcast.6, bf16[224,1024]{1,0:T(8,128)(2,1)} %bitcast.7, bf16[224,1024]{1,0:T(8,128)(2,1)} %bitcast.8, bf16[1024,1536]{1,0:T(8,128)(2,1)} %proj_ref.1, f32[31,1536]{1,0:T(8,128)} %taps_ref.1, ...), custom_call_target="tpu_custom_call" | custom-call | tf_op jit(solution)/shard_map/block/pallas_call | solution.py:508
  225.6 2.0 copy.15

commit v3 on v2

--- a/solution.py
+++ b/solution.py
@@ -101,21 +101,19 @@
 
 
 def slots_of(routes, experts):
-    rows = routes.shape[0]
-    lane = lax.broadcasted_iota(jnp.int32, (rows, 128), 1)
-    hot = [(routes[:, k : k + 1] == lane).astype(F32) for k in range(TOPK)]
+    rows = routes.shape[1]
+    expert = lax.broadcasted_iota(jnp.int32, (experts, rows), 0)
+    hot = [(routes[k : k + 1, :] == expert).astype(F32) for k in range(TOPK)]
     picks = (hot[0] + hot[1]).astype(BF)
-    below = lax.broadcasted_iota(jnp.int32, (rows, rows), 1) < lax.broadcasted_iota(
-        jnp.int32, (rows, rows), 0
+    earlier = lax.broadcasted_iota(jnp.int32, (rows, rows), 0) < lax.broadcasted_iota(
+        jnp.int32, (rows, rows), 1
     )
-    ranks = dot(below.astype(F32).astype(BF), picks)
+    ranks = dot(picks, earlier.astype(F32).astype(BF))
     slots = [
-        routes[:, k : k + 1] * CAP_PAD
-        + jnp.sum(hot[k] * ranks, axis=1, keepdims=True).astype(jnp.int32)
+        routes[k : k + 1, :].astype(F32) * CAP_PAD + jnp.sum(hot[k] * ranks, axis=0, keepdims=True)
         for k in range(TOPK)
     ]
-    places = lax.broadcasted_iota(jnp.int32, (rows, experts * CAP_PAD), 1)
-    return hot, [(slot == places).astype(F32).astype(BF) for slot in slots]
+    return hot, slots
 
 
 GATHER_IDS = 30
@@ -175,32 +173,40 @@
 
     def event(self, n):
         if n == 0:
-            self.start(0, 1, 9, 13)
+            self.start(1, 0, 9, 13)
         elif n == 1:
-            self.receive(0)
-            self.start(16, 23, 20, 26)
-        elif n == 2:
             self.receive(9, 13)
             self.start(10, 14, 2, 6)
+        elif n == 2:
+            self.start(16, 23)
         elif n == 3:
-            self.receive(16, 23, 20, 26)
-            self.start(17, 24, 21, 27)
-        elif n == 4:
             self.receive(10, 14)
             self.start(11, 15, 3, 7)
-        elif n == 5:
-            self.receive(17, 24, 21, 27)
-            self.start(18, 25, 22, 28)
-        elif n == 6:
+        elif n == 4:
             self.receive(11, 15)
             self.start(12, 4, 8)
-        elif n == 7:
-            self.receive(18, 25, 22, 28)
-            self.start(19, 29)
-        elif n == 8:
+            self.receive(0)
+            self.start(20, 26)
+        elif n == 5:
             self.receive(12)
             self.start(5)
+            self.receive(16, 23)
+            self.start(17, 24)
+        elif n == 6:
+            self.receive(20, 26)
+            self.start(21, 27)
+        elif n == 7:
+            self.receive(17, 24)
+            self.start(18, 25)
+        elif n == 8:
+            self.receive(21, 27)
+            self.start(22, 28)
         elif n == 9:
+            self.receive(18, 25)
+            self.start(19)
+            self.receive(22, 28)
+            self.start(29)
+        elif n == 10:
             self.receive(19, 29)
         else:
             self.receive(1, 2, 3, 4, 5, 6, 7, 8)
@@ -240,6 +246,10 @@
     hidden,
     produced,
     returned,
+    placing,
+    picking,
+    hots,
+    numbers,
     gather_send,
     gather_recv,
     load_sem,
@@ -290,9 +300,18 @@
         pack[2 * pair, rows:, :] = jnp.where(low_part, upper, swap(lower)).astype(BF)
         pack[2 * pair + 1, rows:, :] = jnp.where(low_part, swap(upper), lower).astype(BF)
     exchange = spread("tm", tm, pack, held, send_h, recv_h, own_h)
+    gather.event(1)
+    hot, slots = slots_of(routes_ref[...], dp)
+    count = dp * CAP_PAD
+    spots = lax.broadcasted_iota(jnp.int32, (count, rows), 0).astype(F32)
+    placing[...] = ((slots[0] == spots) | (slots[1] == spots)).astype(F32).astype(BF)
+    numbers[...] = jnp.zeros_like(numbers)
+    for k in range(TOPK):
+        hots[k] = hot[k]
+        numbers[k : k + 1, :] = slots[k]
     for copy in exchange:
         copy.wait()
-    gather.event(1)
+    gather.event(2)
 
     scale = scale_ref[me] * 1.4426950408889634
     ends = []
@@ -350,13 +369,13 @@
             att[peer] = deal(peer)
             back(step).start()
 
-        @pl.when(step == 1)
-        def _():
-            gather.event(2)
-
-        @pl.when(step == 13)
+        @pl.when(step == 2)
         def _():
             gather.event(3)
+
+        @pl.when(step == 8)
+        def _():
+            gather.event(4)
 
         return carry
 
@@ -364,12 +383,13 @@
     att[lax.rem(me + 1, tm)] = deal(lax.rem(me + 1, tm))
     back(1).start()
     heads[me] = deal(me)
+    gather.event(5)
     place = me * rows - EDGE + lax.broadcasted_iota(jnp.int32, (wide, 128), 0)
     mark = sum((place >= end).astype(jnp.int32) for end in ends)
     label[...] = jnp.where(place < 0, -1, jnp.where(place >= frames, RECS, mark))
     for distance in range(1, tm):
         back(distance).wait()
-    gather.event(4)
+    gather.event(6)
 
     for top in range(2):
         tiles = []
@@ -407,41 +427,44 @@
                     pl.ds(base + EDGE, group), lanes
                 ] + total[n] / (1.0 + jnp.exp(-total[n]))
 
-        @pl.when(step == 5)
+        @pl.when(step == 6)
         def _():
-            gather.event(5)
+            gather.event(7)
 
         return carry
 
     lax.fori_loop(0, rows // group, conv_rows, 0)
 
     mixed = norm_rows(second[...]).astype(BF)
-    logits = dot(mixed, router_ref[...])
-    hot, places = slots_of(routes_ref[...], dp)
-    powers = jnp.exp(logits)
-    chosen = [jnp.sum(hot[k] * powers, axis=1, keepdims=True) for k in range(TOPK)]
+    powers = jnp.exp(dot(router_ref[...], mixed, ((1,), (1,))))
+    chosen = [jnp.sum(hots[k] * powers, axis=0, keepdims=True) for k in range(TOPK)]
     whole = chosen[0] + chosen[1]
-    gates = [chosen[k] / whole for k in range(TOPK)]
-    both = places[0] + places[1]
+    for k in range(TOPK):
+        numbers[TOPK + k : TOPK + k + 1, :] = chosen[k] / whole
     for expert in range(dp):
-        cut = both[:, expert * CAP_PAD : (expert + 1) * CAP_PAD]
-        outgoing[expert] = dot(cut, mixed, ((0,), (0,))).astype(BF)
+        cut = placing[expert * CAP_PAD : (expert + 1) * CAP_PAD, :]
+        outgoing[expert] = dot(cut, mixed).astype(BF)
     dispatch = spread("dp", dp, outgoing, arrived, send_b, recv_b, own_b)
-    for n in range(6, 10):
-        gather.event(n)
+    gather.event(8)
+    gather.event(9)
+    columns = jnp.transpose(numbers[...])
+    spots = lax.broadcasted_iota(jnp.int32, (rows, count), 1).astype(F32)
+    for k in range(TOPK):
+        picking[k] = (columns[:, k : k + 1] == spots).astype(F32).astype(BF)
+    gates = [columns[:, TOPK + k : TOPK + k + 1] for k in range(TOPK)]
     for copy in dispatch:
         copy.wait()
+    gather.event(10)
 
     units = w_in.shape[0] * w_in.shape[1]
     chunk = w_in.shape[1]
-    count = dp * CAP_PAD
     step_chunks = 4
     for column in range(tm // step_chunks):
         cut = slice(column * step_chunks * chunk, (column + 1) * step_chunks * chunk)
         weights = w_in[column * step_chunks : (column + 1) * step_chunks].reshape(-1, D)
         value = dot(arrived[...].reshape(count, D), weights, ((1,), (1,)))
         hidden[:, cut] = (value / (1.0 + jnp.exp(-value))).astype(BF)
-    gather.event(10)
+    gather.event(11)
     piece = 512
     team = 4
     results = []
@@ -475,7 +498,7 @@
     for column in range(D // piece):
         cut = slice(column * piece, (column + 1) * piece)
         value = returned[:, :, cut].reshape(count, piece)
-        mixture = gates[0] * dot(places[0], value) + gates[1] * dot(places[1], value)
+        mixture = gates[0] * dot(picking[0], value) + gates[1] * dot(picking[1], value)
         out_ref[:, cut] = (second[:, cut] + 0.5 * mixture).astype(BF)
 
 
@@ -503,7 +526,6 @@
     wide = rows + 2 * EDGE
     stacked = rows + rows // 2
     chunk = expert_in.shape[1]
-    wide_router = jnp.pad(router, ((0, 0), (0, 128 - router.shape[1])))
     bf = lambda *shape: pltpu.VMEM(shape, BF)
     out = pl.pallas_call(
         functools.partial(block_kernel, tm, dp),
@@ -530,6 +552,10 @@
             bf(dp * CAP_PAD, tm * chunk),
             bf(dp, CAP_PAD, D),
             bf(dp, CAP_PAD, D),
+            bf(dp * CAP_PAD, rows),
+            bf(TOPK, rows, dp * CAP_PAD),
+            pltpu.VMEM((TOPK, dp, rows), F32),
+            pltpu.VMEM((8, rows), F32),
         ]
         + sems(GATHER_IDS)
         + [pltpu.SemaphoreType.DMA((2,))]
@@ -551,8 +577,8 @@
         value_rows[0],
         out_proj,
         conv_taps,
-        wide_router,
-        routes[0],
+        router.T,
+        routes[0].T,
         expert_in,
         expert_out,
     )

time: 228 us -> 198 us (0.87)
  the two profiles are of different devices: /device:TPU:49 before, /device:TPU:53 now
where the time goes in v3:
time: 198 us
  Pallas kernels  196 us (99%)
  local copies, waits for them, and re-layouts  1.99 us (1%)
    pallas_call x1, Pallas kernels, body(): pl.pallas_call(functools.partial(block_kernel, tm, dp), out_shape=jax.Sha...  196 us

profile of v3, /device:TPU:53, one launch (start us, length us, event | category | flops | bytes accessed | tf_op | source)
XLA Modules:
  0.0 197.8 jit_solution(15946829918340715495)
XLA Ops:
  0.0 195.8 %block.1 = bf16[224,1536]{1,0:T(8,128)(2,1)} custom-call(f32[16]{0:T(128)} %scale_ref.1, s32[1,4]{1,0:T(1,128)} %lengths_ref.1, bf16[224,1024]{1,0:T(8,128)(2,1)} %bitcast.9, bf16[224,1024]{1,0:T(8,128)(2,1)} %bitcast.10, bf16[224,1024]{1,0:T(8,128)(2,1)} %bitcast.11, bf16[1024,1536]{1,0:T(8,128)(2,1)} %proj_ref.1, f32[31,1536]{1,0:T(8,128)} %taps_ref.1, ...), custom_call_target="tpu_custom_call" | custom-call | tf_op jit(solution)/shard_map/block/pallas_call | solution.py:530
  195.8 2.0 %copy.13 = bf16[1,224,1536]{2,1,0:T(8,128)(2,1)} copy(bf16[1,224,1536]{2,1,0:T(8,128)(2,1)} %bitcast.8) | data formatting | bytes 1376256

commit v4 on v3

--- a/solution.py
+++ b/solution.py
@@ -178,35 +178,31 @@
             self.receive(9, 13)
             self.start(10, 14, 2, 6)
         elif n == 2:
-            self.start(16, 23)
+            self.receive(10, 14)
+            self.start(11, 15, 3, 7, 16, 23)
         elif n == 3:
-            self.receive(10, 14)
-            self.start(11, 15, 3, 7)
-        elif n == 4:
             self.receive(11, 15)
             self.start(12, 4, 8)
+        elif n == 4:
             self.receive(0)
             self.start(20, 26)
-        elif n == 5:
             self.receive(12)
             self.start(5)
             self.receive(16, 23)
             self.start(17, 24)
-        elif n == 6:
+        elif n == 5:
             self.receive(20, 26)
             self.start(21, 27)
-        elif n == 7:
+        elif n == 6:
             self.receive(17, 24)
             self.start(18, 25)
-        elif n == 8:
             self.receive(21, 27)
             self.start(22, 28)
-        elif n == 9:
             self.receive(18, 25)
             self.start(19)
             self.receive(22, 28)
             self.start(29)
-        elif n == 10:
+        elif n == 7:
             self.receive(19, 29)
         else:
             self.receive(1, 2, 3, 4, 5, 6, 7, 8)
@@ -300,7 +296,6 @@
         pack[2 * pair, rows:, :] = jnp.where(low_part, upper, swap(lower)).astype(BF)
         pack[2 * pair + 1, rows:, :] = jnp.where(low_part, swap(upper), lower).astype(BF)
     exchange = spread("tm", tm, pack, held, send_h, recv_h, own_h)
-    gather.event(1)
     hot, slots = slots_of(routes_ref[...], dp)
     count = dp * CAP_PAD
     spots = lax.broadcasted_iota(jnp.int32, (count, rows), 0).astype(F32)
@@ -311,7 +306,7 @@
         numbers[k : k + 1, :] = slots[k]
     for copy in exchange:
         copy.wait()
-    gather.event(2)
+    gather.event(1)
 
     scale = scale_ref[me] * 1.4426950408889634
     ends = []
@@ -369,13 +364,13 @@
             att[peer] = deal(peer)
             back(step).start()
 
-        @pl.when(step == 2)
+        @pl.when(step == 5)
+        def _():
+            gather.event(2)
+
+        @pl.when(step == 12)
         def _():
             gather.event(3)
-
-        @pl.when(step == 8)
-        def _():
-            gather.event(4)
 
         return carry
 
@@ -383,13 +378,12 @@
     att[lax.rem(me + 1, tm)] = deal(lax.rem(me + 1, tm))
     back(1).start()
     heads[me] = deal(me)
-    gather.event(5)
     place = me * rows - EDGE + lax.broadcasted_iota(jnp.int32, (wide, 128), 0)
     mark = sum((place >= end).astype(jnp.int32) for end in ends)
     label[...] = jnp.where(place < 0, -1, jnp.where(place >= frames, RECS, mark))
     for distance in range(1, tm):
         back(distance).wait()
-    gather.event(6)
+    gather.event(4)
 
     for top in range(2):
         tiles = []
@@ -427,9 +421,9 @@
                     pl.ds(base + EDGE, group), lanes
                 ] + total[n] / (1.0 + jnp.exp(-total[n]))
 
-        @pl.when(step == 6)
+        @pl.when(step == 3)
         def _():
-            gather.event(7)
+            gather.event(5)
 
         return carry
 
@@ -445,8 +439,7 @@
         cut = placing[expert * CAP_PAD : (expert + 1) * CAP_PAD, :]
         outgoing[expert] = dot(cut, mixed).astype(BF)
     dispatch = spread("dp", dp, outgoing, arrived, send_b, recv_b, own_b)
-    gather.event(8)
-    gather.event(9)
+    gather.event(6)
     columns = jnp.transpose(numbers[...])
     spots = lax.broadcasted_iota(jnp.int32, (rows, count), 1).astype(F32)
     for k in range(TOPK):
@@ -454,17 +447,20 @@
     gates = [columns[:, TOPK + k : TOPK + k + 1] for k in range(TOPK)]
     for copy in dispatch:
         copy.wait()
-    gather.event(10)
 
     units = w_in.shape[0] * w_in.shape[1]
     chunk = w_in.shape[1]
-    step_chunks = 4
-    for column in range(tm // step_chunks):
-        cut = slice(column * step_chunks * chunk, (column + 1) * step_chunks * chunk)
-        weights = w_in[column * step_chunks : (column + 1) * step_chunks].reshape(-1, D)
+    for shift in (0, 1, -1, 2, -2, 3, -3, 4):
+        if shift == 4:
+            gather.event(7)
+        pair = [gather.at(gather.own, shift), gather.at(gather.other, shift)]
+        weights = jnp.concatenate([w_in[one] for one in pair], axis=0)
         value = dot(arrived[...].reshape(count, D), weights, ((1,), (1,)))
-        hidden[:, cut] = (value / (1.0 + jnp.exp(-value))).astype(BF)
-    gather.event(11)
+        value = (value / (1.0 + jnp.exp(-value))).astype(BF)
+        for n, one in enumerate(pair):
+            lanes = pl.ds(pl.multiple_of(one * chunk, chunk), chunk)
+            hidden[:, lanes] = value[:, n * chunk : (n + 1) * chunk]
+    gather.event(8)
     piece = 512
     team = 4
     results = []

time: 198 us -> 192 us (0.970)
  the two profiles are of different devices: /device:TPU:53 before, /device:TPU:1 now
where the time goes in v4:
time: 192 us; the launch traced here: 191 us
  Pallas kernels  189 us (98%)
  local copies, waits for them, and re-layouts  1.99 us (1%)
    pallas_call x1, Pallas kernels, body(): pl.pallas_call(functools.partial(block_kernel, tm, dp), out_shape=jax.Sha...  189 us

profile of v4, /device:TPU:1, one launch (start us, length us, event | category | flops | bytes accessed | tf_op | source)
XLA Modules:
  0.0 190.7 jit_solution(8208962408510125684)
XLA Ops:
  0.0 188.7 %block.1 = bf16[224,1536]{1,0:T(8,128)(2,1)} custom-call(f32[16]{0:T(128)} %scale_ref.1, s32[1,4]{1,0:T(1,128)} %lengths_ref.1, bf16[224,1024]{1,0:T(8,128)(2,1)} %bitcast.9, bf16[224,1024]{1,0:T(8,128)(2,1)} %bitcast.10, bf16[224,1024]{1,0:T(8,128)(2,1)} %bitcast.11, bf16[1024,1536]{1,0:T(8,128)(2,1)} %proj_ref.1, f32[31,1536]{1,0:T(8,128)} %taps_ref.1, ...), custom_call_target="tpu_custom_call" | custom-call | tf_op jit(solution)/shard_map/block/pallas_call | solution.py:526
  188.7 2.0 %copy.13 = bf16[1,224,1536]{2,1,0:T(8,128)(2,1)} copy(bf16[1,224,1536]{2,1,0:T(8,128)(2,1)} %bitcast.8) | data formatting | bytes 1376256

commit v5 on v4

--- a/solution.py
+++ b/solution.py
@@ -176,33 +176,31 @@
             self.start(1, 0, 9, 13)
         elif n == 1:
             self.receive(9, 13)
-            self.start(10, 14, 2, 6)
+            self.start(10, 14, 2, 6, 16, 23)
         elif n == 2:
             self.receive(10, 14)
-            self.start(11, 15, 3, 7, 16, 23)
+            self.start(11, 15, 3, 7)
+            self.receive(0)
+            self.start(20, 26)
+            self.receive(16, 23)
+            self.start(17, 24)
         elif n == 3:
+            self.receive(20, 26)
+            self.start(21, 27)
+        elif n == 4:
             self.receive(11, 15)
             self.start(12, 4, 8)
-        elif n == 4:
-            self.receive(0)
-            self.start(20, 26)
-            self.receive(12)
-            self.start(5)
-            self.receive(16, 23)
-            self.start(17, 24)
-        elif n == 5:
-            self.receive(20, 26)
-            self.start(21, 27)
-        elif n == 6:
             self.receive(17, 24)
             self.start(18, 25)
             self.receive(21, 27)
             self.start(22, 28)
+            self.receive(12)
+            self.start(5)
             self.receive(18, 25)
             self.start(19)
             self.receive(22, 28)
             self.start(29)
-        elif n == 7:
+        elif n == 5:
             self.receive(19, 29)
         else:
             self.receive(1, 2, 3, 4, 5, 6, 7, 8)
@@ -216,8 +214,8 @@
     q_ref,
     k_ref,
     v_ref,
-    proj_ref,
-    taps_ref,
+    proj_hbm,
+    taps_hbm,
     router_ref,
     routes_ref,
     in_ref,
@@ -246,6 +244,8 @@
     picking,
     hots,
     numbers,
+    proj_ref,
+    taps_ref,
     gather_send,
     gather_recv,
     load_sem,
@@ -274,7 +274,11 @@
         pltpu.make_async_copy(in_ref.at[0], w_in.at[me], load_sem.at[0]),
         pltpu.make_async_copy(out_w_ref.at[0], w_out.at[me], load_sem.at[1]),
     ]
-    for load in loads:
+    later = [
+        pltpu.make_async_copy(proj_hbm, proj_ref, load_sem.at[2]),
+        pltpu.make_async_copy(taps_hbm, taps_ref, load_sem.at[3]),
+    ]
+    for load in loads + later:
         load.start()
     for load in loads:
         load.wait()
@@ -364,14 +368,6 @@
             att[peer] = deal(peer)
             back(step).start()
 
-        @pl.when(step == 5)
-        def _():
-            gather.event(2)
-
-        @pl.when(step == 12)
-        def _():
-            gather.event(3)
-
         return carry
 
     lax.fori_loop(0, tm, attend, 0)
@@ -383,7 +379,9 @@
     label[...] = jnp.where(place < 0, -1, jnp.where(place >= frames, RECS, mark))
     for distance in range(1, tm):
         back(distance).wait()
-    gather.event(4)
+    gather.event(2)
+    for load in later:
+        load.wait()
 
     for top in range(2):
         tiles = []
@@ -421,9 +419,9 @@
                     pl.ds(base + EDGE, group), lanes
                 ] + total[n] / (1.0 + jnp.exp(-total[n]))
 
-        @pl.when(step == 3)
+        @pl.when(step == 5)
         def _():
-            gather.event(5)
+            gather.event(3)
 
         return carry
 
@@ -439,7 +437,7 @@
         cut = placing[expert * CAP_PAD : (expert + 1) * CAP_PAD, :]
         outgoing[expert] = dot(cut, mixed).astype(BF)
     dispatch = spread("dp", dp, outgoing, arrived, send_b, recv_b, own_b)
-    gather.event(6)
+    gather.event(4)
     columns = jnp.transpose(numbers[...])
     spots = lax.broadcasted_iota(jnp.int32, (rows, count), 1).astype(F32)
     for k in range(TOPK):
@@ -452,7 +450,7 @@
     chunk = w_in.shape[1]
     for shift in (0, 1, -1, 2, -2, 3, -3, 4):
         if shift == 4:
-            gather.event(7)
+            gather.event(5)
         pair = [gather.at(gather.own, shift), gather.at(gather.other, shift)]
         weights = jnp.concatenate([w_in[one] for one in pair], axis=0)
         value = dot(arrived[...].reshape(count, D), weights, ((1,), (1,)))
@@ -460,7 +458,7 @@
         for n, one in enumerate(pair):
             lanes = pl.ds(pl.multiple_of(one * chunk, chunk), chunk)
             hidden[:, lanes] = value[:, n * chunk : (n + 1) * chunk]
-    gather.event(8)
+    gather.event(6)
     piece = 512
     team = 4
     results = []
@@ -526,7 +524,7 @@
     out = pl.pallas_call(
         functools.partial(block_kernel, tm, dp),
         out_shape=jax.ShapeDtypeStruct((rows, D), BF),
-        in_specs=[smem_spec()] * 2 + [vmem_spec()] * 7 + [any_spec()] * 2,
+        in_specs=[smem_spec()] * 2 + [vmem_spec()] * 3 + [any_spec()] * 2 + [vmem_spec()] * 2 + [any_spec()] * 2,
         out_specs=vmem_spec(),
         scratch_shapes=[
             bf(tm, stacked, 128),
@@ -552,9 +550,11 @@
             bf(TOPK, rows, dp * CAP_PAD),
             pltpu.VMEM((TOPK, dp, rows), F32),
             pltpu.VMEM((8, rows), F32),
+            bf(*out_proj.shape),
+            pltpu.VMEM(conv_taps.shape, F32),
         ]
         + sems(GATHER_IDS)
-        + [pltpu.SemaphoreType.DMA((2,))]
+        + [pltpu.SemaphoreType.DMA((4,))]
         + sems(tm - 1)
         + [pltpu.SemaphoreType.DMA]
         + sems(tm - 1)

time: 192 us -> 206 us (1.073)
  the two profiles are of different devices: /device:TPU:1 before, /device:TPU:7 now
where the time goes in v5:
time: 206 us
  Pallas kernels  204 us (99%)
    pallas_call x1, Pallas kernels, body(): pl.pallas_call(functools.partial(block_kernel, tm, dp), out_shape=jax.Sha...  204 us

profile of v5, /device:TPU:7, one launch (start us, length us, event | category | flops | bytes accessed | tf_op | source)
XLA Modules:
  0.0 206.0 jit_solution(3853170889304032512)
XLA Ops:
  0.0 204.0 %block.1 = bf16[224,1536]{1,0:T(8,128)(2,1)} custom-call(f32[16]{0:T(128)} %scale_ref.1, s32[1,4]{1,0:T(1,128)} %lengths_ref.1, bf16[224,1024]{1,0:T(8,128)(2,1)} %bitcast.9, bf16[224,1024]{1,0:T(8,128)(2,1)} %bitcast.10, bf16[224,1024]{1,0:T(8,128)(2,1)} %bitcast.11, bf16[1024,1536]{1,0:T(8,128)(2,1)} %proj_hbm.1, f32[31,1536]{1,0:T(8,128)} %taps_hbm.1, ...), custom_call_target="tpu_custom_call" | custom-call | tf_op jit(solution)/shard_map/block/pallas_call | solution.py:524
  204.0 2.0 copy.13

commit v6 on v4

--- a/solution.py
+++ b/solution.py
@@ -182,15 +182,16 @@
             self.start(11, 15, 3, 7, 16, 23)
         elif n == 3:
             self.receive(11, 15)
-            self.start(12, 4, 8)
-        elif n == 4:
+            self.start(12)
             self.receive(0)
             self.start(20, 26)
-            self.receive(12)
-            self.start(5)
+        elif n == 4:
+            self.start(4, 8)
             self.receive(16, 23)
             self.start(17, 24)
         elif n == 5:
+            self.receive(12)
+            self.start(5)
             self.receive(20, 26)
             self.start(21, 27)
         elif n == 6:
@@ -216,8 +217,8 @@
     q_ref,
     k_ref,
     v_ref,
-    proj_ref,
-    taps_ref,
+    proj_hbm,
+    taps_hbm,
     router_ref,
     routes_ref,
     in_ref,
@@ -246,6 +247,8 @@
     picking,
     hots,
     numbers,
+    proj_ref,
+    taps_ref,
     gather_send,
     gather_recv,
     load_sem,
@@ -274,7 +277,11 @@
         pltpu.make_async_copy(in_ref.at[0], w_in.at[me], load_sem.at[0]),
         pltpu.make_async_copy(out_w_ref.at[0], w_out.at[me], load_sem.at[1]),
     ]
-    for load in loads:
+    later = [
+        pltpu.make_async_copy(proj_hbm, proj_ref, load_sem.at[2]),
+        pltpu.make_async_copy(taps_hbm, taps_ref, load_sem.at[3]),
+    ]
+    for load in loads + later:
         load.start()
     for load in loads:
         load.wait()
@@ -378,12 +385,15 @@
     att[lax.rem(me + 1, tm)] = deal(lax.rem(me + 1, tm))
     back(1).start()
     heads[me] = deal(me)
+    gather.event(4)
     place = me * rows - EDGE + lax.broadcasted_iota(jnp.int32, (wide, 128), 0)
     mark = sum((place >= end).astype(jnp.int32) for end in ends)
     label[...] = jnp.where(place < 0, -1, jnp.where(place >= frames, RECS, mark))
     for distance in range(1, tm):
         back(distance).wait()
-    gather.event(4)
+    gather.event(5)
+    for load in later:
+        load.wait()
 
     for top in range(2):
         tiles = []
@@ -420,10 +430,6 @@
                 second[pl.ds(base, group), lanes] = first_s[
                     pl.ds(base + EDGE, group), lanes
                 ] + total[n] / (1.0 + jnp.exp(-total[n]))
-
-        @pl.when(step == 3)
-        def _():
-            gather.event(5)
 
         return carry
 
@@ -526,7 +532,7 @@
     out = pl.pallas_call(
         functools.partial(block_kernel, tm, dp),
         out_shape=jax.ShapeDtypeStruct((rows, D), BF),
-        in_specs=[smem_spec()] * 2 + [vmem_spec()] * 7 + [any_spec()] * 2,
+        in_specs=[smem_spec()] * 2 + [vmem_spec()] * 3 + [any_spec()] * 2 + [vmem_spec()] * 2 + [any_spec()] * 2,
         out_specs=vmem_spec(),
         scratch_shapes=[
             bf(tm, stacked, 128),
@@ -552,9 +558,11 @@
             bf(TOPK, rows, dp * CAP_PAD),
             pltpu.VMEM((TOPK, dp, rows), F32),
             pltpu.VMEM((8, rows), F32),
+            bf(*out_proj.shape),
+            pltpu.VMEM(conv_taps.shape, F32),
         ]
         + sems(GATHER_IDS)
-        + [pltpu.SemaphoreType.DMA((2,))]
+        + [pltpu.SemaphoreType.DMA((4,))]
         + sems(tm - 1)
         + [pltpu.SemaphoreType.DMA]
         + sems(tm - 1)

time: 192 us -> 194 us (1.010)
  Pallas kernels: 189 us -> 192 us
    pallas_call x1, Pallas kernels: 189 us -> 192 us  [body(): pl.pallas_call(functools.partial(block_kernel, tm, dp), out_shape=jax.Sha...]
where the time goes in v6:
time: 194 us
  Pallas kernels  192 us (99%)
  local copies, waits for them, and re-layouts  1.99 us (1%)
    pallas_call x1, Pallas kernels, body(): pl.pallas_call(functools.partial(block_kernel, tm, dp), out_shape=jax.Sha...  192 us

profile of v6, /device:TPU:1, one launch (start us, length us, event | category | flops | bytes accessed | tf_op | source)
XLA Modules:
  0.0 193.6 jit_solution(12458936691246722173)
XLA Ops:
  0.0 191.6 %block.1 = bf16[224,1536]{1,0:T(8,128)(2,1)} custom-call(f32[16]{0:T(128)} %scale_ref.1, s32[1,4]{1,0:T(1,128)} %lengths_ref.1, bf16[224,1024]{1,0:T(8,128)(2,1)} %bitcast.9, bf16[224,1024]{1,0:T(8,128)(2,1)} %bitcast.10, bf16[224,1024]{1,0:T(8,128)(2,1)} %bitcast.11, bf16[1024,1536]{1,0:T(8,128)(2,1)} %proj_hbm.1, f32[31,1536]{1,0:T(8,128)} %taps_hbm.1, ...), custom_call_target="tpu_custom_call" | custom-call | tf_op jit(solution)/shard_map/block/pallas_call | solution.py:532
  191.6 2.0 %copy.13 = bf16[1,224,1536]{2,1,0:T(8,128)(2,1)} copy(bf16[1,224,1536]{2,1,0:T(8,128)(2,1)} %bitcast.8) | data formatting | bytes 1376256

commit v7 on v6

--- a/solution.py
+++ b/solution.py
@@ -182,11 +182,10 @@
             self.start(11, 15, 3, 7, 16, 23)
         elif n == 3:
             self.receive(11, 15)
-            self.start(12)
+            self.start(12, 4, 8)
             self.receive(0)
             self.start(20, 26)
         elif n == 4:
-            self.start(4, 8)
             self.receive(16, 23)
             self.start(17, 24)
         elif n == 5:
@@ -194,9 +193,10 @@
             self.start(5)
             self.receive(20, 26)
             self.start(21, 27)
-        elif n == 6:
+        elif n == 9:
             self.receive(17, 24)
             self.start(18, 25)
+        elif n == 6:
             self.receive(21, 27)
             self.start(22, 28)
             self.receive(18, 25)
@@ -430,6 +430,10 @@
                 second[pl.ds(base, group), lanes] = first_s[
                     pl.ds(base + EDGE, group), lanes
                 ] + total[n] / (1.0 + jnp.exp(-total[n]))
+
+        @pl.when(step == 4)
+        def _():
+            gather.event(9)
 
         return carry
 

time: 194 us -> 196 us (1.010); the launches traced: 194 us -> 193 us
  no operation moved by 1% of the time
where the time goes in v7:
time: 196 us; the launch traced here: 193 us
  Pallas kernels  191 us (97%)
  local copies, waits for them, and re-layouts  1.99 us (1%)
    pallas_call x1, Pallas kernels, body(): pl.pallas_call(functools.partial(block_kernel, tm, dp), out_shape=jax.Sha...  191 us

profile of v7, /device:TPU:1, one launch (start us, length us, event | category | flops | bytes accessed | tf_op | source)
XLA Modules:
  0.0 193.2 jit_solution(17819667021649200078)
XLA Ops:
  0.0 191.2 %block.1 = bf16[224,1536]{1,0:T(8,128)(2,1)} custom-call(f32[16]{0:T(128)} %scale_ref.1, s32[1,4]{1,0:T(1,128)} %lengths_ref.1, bf16[224,1024]{1,0:T(8,128)(2,1)} %bitcast.9, bf16[224,1024]{1,0:T(8,128)(2,1)} %bitcast.10, bf16[224,1024]{1,0:T(8,128)(2,1)} %bitcast.11, bf16[1024,1536]{1,0:T(8,128)(2,1)} %proj_hbm.1, f32[31,1536]{1,0:T(8,128)} %taps_hbm.1, ...), custom_call_target="tpu_custom_call" | custom-call | tf_op jit(solution)/shard_map/block/pallas_call | solution.py:536
  191.2 2.0 %copy.13 = bf16[1,224,1536]{2,1,0:T(8,128)(2,1)} copy(bf16[1,224,1536]{2,1,0:T(8,128)(2,1)} %bitcast.8) | data formatting | bytes 1376256
